TPU v7x, 256 devices: a whole 4x4x8 slice. The times are simulated.
256 devices in a mesh: ctx: 16 (over y_hi, z), tp: 16 (over x, y_lo, core).
Axes of the slice: x: 4, y: 4 (y_hi: 2, y_lo: 2; y = y_hi * 2 + y_lo), z: 8, core: 2. Of those that a mesh axis runs over, the one named last changes fastest.
Arguments:
- hidden_in: bfloat16 [8192, 8192], P('ctx', 'tp'), may hold values from -30 to 30
- norm_gain: bfloat16 [8192], P('tp'), may hold values from 0.099609375 to 1.8984375
- w_query: bfloat16 [8192, 4096], P(None, 'tp'), may hold values from -1 to 1
- w_key: bfloat16 [8192, 1024], P(None, 'tp'), may hold values from -1 to 1
- w_value: bfloat16 [8192, 1024], P(None, 'tp'), may hold values from -0.0625 to 0.0625
- sign_bits: int32 [32, 128], P('tp'), may hold values from 0 to 1
- w_out: bfloat16 [4096, 8192], P(None, 'tp'), may hold values from -1 to 1
- teacher: bfloat16 [8192, 8192], P('ctx', 'tp'), may hold values from -30 to 30
Outputs:
- student: bfloat16 [8192, 8192], P('ctx', 'tp')
- row_loss: float32 [8192], P('ctx')
Inputs may be any that keep to these rules, and one draw needn't show every extreme that they name: `sign_bits`: 1 stands for the sign +1 and 0 for -1.
All inputs are finite; a program needn't handle non-finite values.
Results may differ from a plain program's by a relative error of at most 0.012.
The roundings to bfloat16 on the way count: a program that leaves them out, or rounds other values in their place, can miss the bound.
Values may be sent and summed in bfloat16 or wider, within the bound.
A program may use at most 128 MiB of HBM per device.

v0:
```python
import jax
import jax.numpy as jnp
from jax import lax
from jax.sharding import PartitionSpec as P

D = 8192
QH = 32
HD = 128
GROUP = 128


EPS_IN = 1e-05
EPS_OUT = 1e-06
CLIP_RATIO = 0.9
FAR_BELOW = -1e30


def swapped(shard, axis, distance):
    return lax.ppermute(shard, axis, [(i, i ^ 1 << distance) for i in range(lax.axis_size(axis))])


def clip_groups(values):
    lead_shape = values.shape[:-1]
    width = values.shape[-1]
    grouped = values.reshape(lead_shape + (width // GROUP, GROUP))
    limit = CLIP_RATIO * jnp.max(jnp.abs(grouped), axis=-1, keepdims=True)
    return jnp.clip(grouped, -limit, limit).reshape(values.shape)


def hadamard(order, dtype):
    index_row = jnp.arange(order, dtype=jnp.int32)
    both_bits = index_row[:, None] & index_row[None, :]
    parity = jnp.zeros_like(both_bits)
    for bit_index in range(max(order - 1, 1).bit_length()):
        parity = parity ^ both_bits >> bit_index & 1
    return (1 - 2 * parity).astype(dtype)


def body(hidden_in, norm_gain, w_query, w_key, w_value, sign_bits, w_out, teacher):
    rows_here = hidden_in.shape[0]
    whole_rows, whole_gain = (
        lax.all_gather(hidden_in, "tp", axis=1, tiled=True),
        lax.all_gather(norm_gain, "tp", axis=0, tiled=True),
    )
    inputs = whole_rows.astype(jnp.float32)
    mean_sq = jnp.mean(inputs * inputs, axis=-1, keepdims=True)
    normed = inputs * lax.rsqrt(mean_sq + EPS_IN) * whole_gain.astype(jnp.float32)
    quantized = clip_groups(normed).astype(jnp.bfloat16)
    queries = jnp.dot(quantized, w_query, preferred_element_type=jnp.float32).astype(jnp.bfloat16)
    key_cols = jnp.dot(quantized, w_key, preferred_element_type=jnp.float32).astype(jnp.bfloat16)
    value_cols = jnp.dot(quantized, w_value, preferred_element_type=jnp.float32).astype(
        jnp.bfloat16
    )
    key_vals = (key_cols, value_cols)
    partner = swapped((key_vals[0], key_vals[1]), "tp", 0)
    upper_half = lax.axis_index("tp") >> 0 & 1 == 1
    key_vals = tuple(
        (
            jnp.where(
                upper_half,
                jnp.concatenate([remote, nearby], axis=1),
                jnp.concatenate([nearby, remote], axis=1),
            )
            for nearby, remote in zip(key_vals, partner)
        )
    )
    heads_here = w_query.shape[1] // HD
    kv_here = key_vals[0].shape[1] // HD
    group_size = heads_here // kv_here
    grouped_queries = queries.reshape(rows_here, kv_here, group_size, HD)
    query_pos = lax.axis_index("ctx") * rows_here + jnp.arange(rows_here, dtype=jnp.int32)
    score_scale = HD ** (-0.5)
    initial = (
        jnp.full((kv_here, group_size, rows_here), FAR_BELOW, jnp.float32),
        jnp.zeros((kv_here, group_size, rows_here), jnp.float32),
        jnp.zeros((kv_here, group_size, rows_here, HD), jnp.float32),
    )
    block_keys = lax.all_gather(key_vals[0], "ctx", axis=0, tiled=True)
    block_values = lax.all_gather(key_vals[1], "ctx", axis=0, tiled=True)
    block_count = block_keys.shape[0] // rows_here

    def advance(index, state):
        highest, weight_sum, accum = state
        begin = index * rows_here
        keys_now = lax.dynamic_slice_in_dim(block_keys, begin, rows_here, 0).reshape(
            rows_here, kv_here, HD
        )
        values_now = lax.dynamic_slice_in_dim(block_values, begin, rows_here, 0).reshape(
            rows_here, kv_here, HD
        )
        key_pos = begin + jnp.arange(rows_here, dtype=jnp.int32)
        scores = (
            jnp.einsum(
                "qkgd,nkd->kgqn", grouped_queries, keys_now, preferred_element_type=jnp.float32
            )
            * score_scale
        )
        causal = key_pos[None, :] <= query_pos[:, None]
        masked = jnp.where(causal, scores, FAR_BELOW)
        new_highest = jnp.maximum(highest, jnp.max(masked, axis=-1))
        decay = jnp.exp(highest - new_highest)
        weights = jnp.where(causal, jnp.exp(masked - new_highest[..., None]), 0.0)
        weight_sum = decay * weight_sum + jnp.sum(weights, axis=-1)
        mixed = jnp.einsum(
            "kgqn,nkd->kgqd",
            weights.astype(jnp.bfloat16),
            values_now,
            preferred_element_type=jnp.float32,
        )
        accum = decay[..., None] * accum + mixed
        return (new_highest, weight_sum, accum)

    highest, weight_sum, accum = lax.fori_loop(0, block_count, advance, initial)
    attended = (
        (accum / weight_sum[..., None])
        .transpose(2, 0, 1, 3)
        .reshape(rows_here, heads_here, HD)
        .astype(jnp.bfloat16)
    )
    signs_here = (2 * sign_bits - 1).astype(jnp.float32)
    signed = (attended * signs_here.astype(jnp.bfloat16)[None, :, :]).reshape(
        rows_here, heads_here * HD
    )
    signed_all = lax.all_gather(signed, "tp", axis=1, tiled=True).reshape(rows_here, QH, HD)
    whole_mix = hadamard(QH, jnp.bfloat16)
    rotated_whole = jnp.einsum(
        "hg,tgd->thd", whole_mix, signed_all, preferred_element_type=jnp.float32
    ) * QH ** (-0.5)
    rotated_all = clip_groups(rotated_whole.reshape(rows_here, QH * HD)).astype(jnp.bfloat16)
    branch = jnp.dot(rotated_all, w_out, preferred_element_type=jnp.float32)
    target = teacher.astype(jnp.float32)
    branch_sq = lax.psum(jnp.sum(branch * branch, axis=-1), "tp")
    inverse = lax.rsqrt(branch_sq / D + EPS_OUT)
    normal_rows = branch * inverse[:, None]
    difference = normal_rows - target
    row_loss = lax.psum(jnp.sum(difference * difference, axis=-1), "tp") / D
    return (normal_rows.astype(jnp.bfloat16), row_loss)


def solution(mesh):
    in_specs = (
        P("ctx", "tp"),
        P("tp"),
        P(None, "tp"),
        P(None, "tp"),
        P(None, "tp"),
        P("tp", None),
        P(None, "tp"),
        P("ctx", "tp"),
    )
    out_specs = (P("ctx", "tp"), P("ctx"))
    return jax.shard_map(body, mesh=mesh, in_specs=in_specs, out_specs=out_specs, check_vma=False)
```

profile of v0, /device:TPU:17, one launch (start us, length us, event | category | flops | bytes accessed | tf_op | source)
XLA Modules:
  0.0 539.9 jit_solution(6028524829673039888)
XLA Ops:
  8.6 20.1 %all-gather = bf16[16,1,512]{2,1,0:T(2,128)(2,1)S(1)} all-gather(bf16[1,1,512]{2,1,0:T(2,128)(2,1)S(1)} %reshape.104), channel_id=1, replica_groups=mesh['ctx'=16,'tp'=16] {'tp'}, dimensions={0}, use_global_device_ids=true | all-gather | bytes 17408 | tf_op jit(solution)/shard_map/all_gather | solution.py:43
  28.7 38.8 %all-gather.6.cloned.1.call-done = bf16[512,8192]{1,0:T(8,128)(2,1)} async-done(((bf16[512,512]{1,0:T(8,128)(2,1)}), bf16[512,8192]{1,0:T(8,128)(2,1)}) %all-gather.6.cloned.1.call-update) | async-done | bytes 8388624 | tf_op jit(solution)/shard_map/all_gather | solution.py:42
  67.5 5.1 fusion.25
  72.6 12.0 %fusion.29 = f32[64,8,64,128]{3,1,2,0:T(8,128)} fusion(bf16[512,8192]{1,0:T(8,128)(2,1)} %all-gather.6.cloned.1.call-done, f32[8192]{0:T(1024)S(1)} %bitcast.115, f32[512]{0:T(512)S(1)} %add_rsqrt_fusion.1), kind=kLoop, calls=%fused_computation.41 | loop fusion | flops 16777216 | bytes 25200640
  84.7 14.1 %copy.36 = f32[64,8,64,128]{3,2,1,0:T(8,128)} copy(f32[64,8,64,128]{3,1,2,0:T(8,128)} %fusion.29) | data formatting | bytes 33554432
  98.8 8.2 %reduce_max.31 = f32[512,64]{1,0:T(8,128)S(1)} reduce(f32[512,64,128]{2,1,0:T(8,128)} %bitcast.108, f32[]{:T(128)} %constant.90.clone.1), dimensions={2}, to_apply=%region_1.0 | reduce | flops 4161536 | bytes 16908292 | tf_op jit(solution)/shard_map/reduce_max | solution.py:26
  107.0 6.3 %min.28 = bf16[512,64,128]{2,1,0:T(8,128)(2,1)S(1)} broadcast(bf16[512,64]{1,0:T(8,128)(2,1)S(1)} %get-tuple-element.230), dimensions={0,1} | broadcast | bytes 8454144 | tf_op jit(solution)/shard_map/jit(clip)/min | solution.py:27
  113.3 6.3 %max.35 = bf16[512,64,128]{2,1,0:T(8,128)(2,1)S(1)} broadcast(bf16[512,64]{1,0:T(8,128)(2,1)S(1)} %get-tuple-element.231), dimensions={0,1} | broadcast | bytes 8454144 | tf_op jit(solution)/shard_map/jit(clip)/max | solution.py:27
  119.6 35.1 %fusion.31 = bf16[512,8192]{1,0:T(8,128)(2,1)S(1)} fusion(bf16[512,8192]{1,0:T(8,128)(2,1)S(1)} %bitcast.107, bf16[64,8,64,128]{3,2,1,0:T(8,128)(2,1)S(1)} %bitcast.110, bf16[64,8,64,128]{3,2,1,0:T(8,128)(2,1)S(1)} %bitcast.109, f32[8192]{0:T(1024)S(1)} %bitcast.116, f32[512]{0:T(512)S(1)} %add_rsqrt_fusion.1), kind=kLoop, calls=%fused_computation.43 | loop fusion | flops 33554432 | bytes 33589248 | tf_op jit(solution)/shard_map/convert_element_type | solution.py:48
  159.9 10.9 %all-gather.8.cloned.1.call-start = ((), (), s32[]{:S(2)}) async-start(), calls=%async_computation.1 | async-start | bytes 2228224 | tf_op jit(solution)/shard_map/all_gather | solution.py:78
  170.9 6.1 %convolution_convert_fusion.2 = bf16[512,64]{0,1:T(8,128)(2,1)S(1)} fusion(bf16[512,8192]{1,0:T(8,128)(2,1)} %copy-done.2, bf16[8192,64]{0,1:T(8,128)(2,1)S(1)} %copy-done.3), kind=kOutput, calls=%fused_computation.51 | convolution fusion | flops 536903680 | bytes 9502720 | tf_op jit(solution)/shard_map/dot_general | solution.py:50
  179.2 7.0 %convolution_convert_fusion = bf16[512,256]{0,1:T(8,128)(2,1)S(1)} fusion(bf16[512,8192]{1,0:T(8,128)(2,1)} %copy-done.2, bf16[8192,256]{1,0:T(8,128)(2,1)} %param.12), kind=kOutput, calls=%fused_computation.49 | convolution fusion | flops 2147614720 | bytes 12845056 | tf_op jit(solution)/shard_map/dot_general | solution.py:49
  186.3 52.2 %all-gather.10.cloned.1.call-done = bf16[8192,128]{0,1:T(8,128)(2,1)} async-done(((bf16[512,128]{0,1:T(8,128)(2,1)}), bf16[8192,128]{0,1:T(8,128)(2,1)}) %all-gather.10.cloned.1.call-update) | async-done | bytes 2097168 | tf_op jit(solution)/shard_map/all_gather | solution.py:79
  238.5 83.8 %all-gather.8.cloned.1.call-done = bf16[8192,128]{0,1:T(8,128)(2,1)} async-done(((bf16[512,128]{0,1:T(8,128)(2,1)}), bf16[8192,128]{0,1:T(8,128)(2,1)}) %all-gather.8.cloned.1.call-update) | async-done | bytes 2097168 | tf_op jit(solution)/shard_map/all_gather | solution.py:78
  322.3 82.5 %while.18 = (s32[]{:T(128)}, f32[1,2,512]{2,1,0:T(2,128)S(1)}, f32[1,2,512]{2,1,0:T(2,128)S(1)}, f32[1,2,512,128]{3,2,1,0:T(8,128)}, bf16[8192,128]{0,1:T(8,128)...) while((s32[]{:T(128)}, f32[1,2,512]{2,1,0:T(2,128)S(1)}, ...), condition=%wide.region_5.6_spmd.clone, body=%wide.region_2.5_spmd.clone.sunk | while | flops 275913728 | bytes 8986815 | solution.py:113
  329.0 2.8 fusion.70
  339.3 2.8 fusion.70
  408.2 42.1 %all-gather.12.cloned.1.call-done = bf16[512,4096]{0,1:T(8,128)(2,1)} async-done(((bf16[512,256]{0,1:T(8,128)(2,1)}), bf16[512,4096]{0,1:T(8,128)(2,1)}) %all-gather.12.cloned.1.call-update) | async-done | bytes 4194320 | tf_op jit(solution)/shard_map/all_gather | solution.py:124
  450.3 7.9 %copy.33 = bf16[512,32,128]{2,1,0:T(8,128)(2,1)} copy(bf16[512,32,128]{0,2,1:T(8,128)(2,1)} %bitcast.112) | data formatting | bytes 8388608 | tf_op jit(solution)/shard_map/reshape | solution.py:124
  458.2 4.7 abs_reduce_fusion
  463.0 9.5 %minimum_convert_fusion = bf16[512,128,32]{1,2,0:T(8,128)(2,1)S(1)} fusion(f32[512,128,32]{1,2,0:T(8,128)S(1)} %get-tuple-element.233, bf16[512,32]{1,0:T(8,128)(2,1)S(1)} %get-tuple-element.229, bf16[512,32]{1,0:T(8,128)(2,1)S(1)} %get-tuple-element.228), kind=kLoop, calls=%fused_computation.44 | loop fusion | flops 12582912 | bytes 12648448 | tf_op jit(solution)/shard_map/convert_element_type | solution.py:129
  472.6 2.9 multiply_reduce_fusion.1
  475.6 26.8 %psum.14 = f32[512]{0:T(512)S(1)} all-reduce(f32[512]{0:T(512)S(1)} %get-tuple-element.234), channel_id=1, replica_groups=mesh['ctx'=16,'tp'=16] {'tp'}, use_global_device_ids=true, to_apply=%region_8.9 | all-reduce | flops 512 | bytes 4096 | tf_op jit(solution)/shard_map/psum | solution.py:132
  503.6 29.0 %psum.15 = f32[512]{0:T(512)S(1)} all-reduce(f32[512]{0:T(512)S(1)} %get-tuple-element.226), channel_id=1, replica_groups=mesh['ctx'=16,'tp'=16] {'tp'}, use_global_device_ids=true, to_apply=%region_10.11 | all-reduce | flops 512 | bytes 4096 | tf_op jit(solution)/shard_map/psum | solution.py:136
  (175 shorter events, 90.1 us)
Async XLA Ops:
  7.2 147.5 %copy-start = (bf16[8192,64]{0,1:T(8,128)(2,1)S(1)}, bf16[8192,64]{0,1:T(8,128)(2,1)}, u32[]{:S(2)}) copy-start(bf16[8192,64]{0,1:T(8,128)(2,1)} %param.14) | copy-start | bytes 3145732
  7.2 60.3 %all-gather.6.cloned.1.call-start = ((), (), s32[]{:S(2)}) async-start(), calls=%async_computation | async-start | bytes 8912896 | tf_op jit(solution)/shard_map/all_gather | solution.py:42
  7.9 230.6 %all-gather.10.cloned.1.call-start = ((), (), s32[]{:S(2)}) async-start(), calls=%async_computation.2 | async-start | bytes 2228224 | tf_op jit(solution)/shard_map/all_gather | solution.py:79
  107.0 12.6 %slice-start = ((s8[8388608]{0:T(1024)(128)(4,1)}), s8[4194304]{0:T(1024)(128)(4,1)S(1)}, s32[]{:S(2)}) async-start(s8[8388608]{0:T(1024)(128)(4,1)} %bitcast.106), calls=%async_computation.4 | async-start | bytes 8388608
  113.3 6.3 %slice-start.1 = ((s8[8388608]{0:T(1024)(128)(4,1)}), s8[4194304]{0:T(1024)(128)(4,1)S(1)}, s32[]{:S(2)}) async-start(s8[8388608]{0:T(1024)(128)(4,1)} %bitcast.106), calls=%async_computation.5 | async-start | bytes 8388608
  154.7 3.2 copy-start.2
  154.7 16.1 %copy-start.3 = (bf16[8192,64]{0,1:T(8,128)(2,1)S(1)}, bf16[8192,64]{0,1:T(8,128)(2,1)}, u32[]{:S(2)}) copy-start(bf16[8192,64]{0,1:T(8,128)(2,1)} %param.13) | copy-start | bytes 3145732
  157.9 1.3 collective-permute-start.1
  159.9 19.3 %copy-start.5 = (s32[2,128]{1,0:T(2,128)S(1)}, s32[2,128]{1,0:T(2,128)}, u32[]{:S(2)}) copy-start(s32[2,128]{1,0:T(2,128)} %param.15) | copy-start | bytes 3076
  159.9 162.4 %all-gather.8.cloned.1.call-start = ((), (), s32[]{:S(2)}) async-start(), calls=%async_computation.1 | async-start | bytes 2228224 | tf_op jit(solution)/shard_map/all_gather | solution.py:78
  177.0 1.3 collective-permute-start
  179.1 271.3 %all-gather.12.cloned.1.call-start = ((), (), s32[]{:S(2)}) async-start(), calls=%async_computation.3 | async-start | bytes 4456448 | tf_op jit(solution)/shard_map/all_gather | solution.py:124
  463.0 9.6 %copy-start.4 = (bf16[4096,512]{1,0:T(8,128)(2,1)S(1)}, bf16[4096,512]{1,0:T(8,128)(2,1)}, u32[]{:S(2)}) copy-start(bf16[4096,512]{1,0:T(8,128)(2,1)} %param.16) | copy-start | bytes 12582916
  472.6 60.6 %copy-start.1 = (bf16[8192,64]{0,1:T(8,128)(2,1)S(1)}, bf16[8192,64]{0,1:T(8,128)(2,1)}, u32[]{:S(2)}) copy-start(bf16[8192,64]{0,1:T(8,128)(2,1)} %param.14) | copy-start | bytes 3145732
Sparse Core Ops, SparseCore 0:
  9.8 57.6 all-gather.5
  160.0 78.4 all-gather.9
  241.0 81.2 all-gather.7
  407.0 43.2 all-gather.11
where the time goes:
time: 549 us; the launch traced here: 540 us
  waiting for transfers between devices  220 us (40%)
  matrix products  91.8 us (17%)
  other arithmetic  86.2 us (16%)
  blocking collectives  75.9 us (14%)
  local copies, waits for them, and re-layouts  39.5 us (7%)
  between operations  14.2 us (3%)
  starting transfers between devices  11.7 us (2%)
    all_gather x1, waiting for transfers between devices, body(): block_keys = lax.all_gather(key_vals[0], 'ctx', axis=0, tiled=True)  83.8 us
    all_gather x1, waiting for transfers between devices, body(): block_values = lax.all_gather(key_vals[1], 'ctx', axis=0, tiled=True)  52.2 us
    dot_general x16, matrix products, advance(): jnp.einsum('kgqn,nkd->kgqd', weights.astype(jnp.bfloat16), values_now, pr...  44.5 us
    all_gather x1, waiting for transfers between devices, body(): lax.all_gather(signed, 'tp', axis=1, tiled=True).reshape(rows_here, QH, HD)  42.1 us
    all_gather x1, waiting for transfers between devices, body(): lax.all_gather(hidden_in, 'tp', axis=1, tiled=True)  38.8 us
    convert_element_type x1, other arithmetic, body(): quantized = clip_groups(normed).astype(jnp.bfloat16)  35.1 us
    psum x1, blocking collectives, body(): row_loss = lax.psum(jnp.sum(difference * difference, axis=-1), 'tp') / D  29 us
    psum x1, blocking collectives, body(): branch_sq = lax.psum(jnp.sum(branch * branch, axis=-1), 'tp')  26.8 us
  transfers between devices with their start and end apart: 6, of which 6 were waited for; matrix products, arithmetic and copies ran while one was open for 3% of the time, Pallas kernels for 0%

commit v1 on v0

v1 whole, which is shorter than its diff:
```python
import functools

import jax
import jax.numpy as jnp
from jax import lax
from jax.experimental import pallas as pl
from jax.experimental.pallas import tpu as pltpu
from jax.sharding import PartitionSpec as P

MESH = pl.DeviceIdType.MESH
F32 = jnp.float32
BF16 = jnp.bfloat16

D = 8192
QH = 32
HD = 128
ROWS = 512
TP = 16
WIDTH = D // TP
EPS_IN = 1e-05
EPS_OUT = 1e-06
CLIP_RATIO = 0.9
FAR_BELOW = -1e30
LOG2E = 1.4426950408889634
VMEM_LIMIT = 62 * 1024 * 1024


def tp_id(x, y, core):
    return lax.rem(x + 8, 4) * 4 + y * 2 + core


def tp_coords():
    me = lax.axis_index("tp")
    return me // 4, lax.rem(me // 2, 2), lax.rem(me, 2)


class Gather:
    def __init__(self, own, buf, send, recv):
        self.own, self.buf, self.send, self.recv = own, buf, send, recv
        x, y, core = tp_coords()
        self.core = core
        self.me = tp_id(x, y, core)
        self.right, self.left = tp_id(x + 1, y, core), tp_id(x - 1, y, core)
        self.across, self.mate = tp_id(x, 1 - y, core), tp_id(x, y, 1 - core)
        self.slots = [
            tp_id(x - 1, y, core),
            tp_id(x + 1, y, core),
            tp_id(x, 1 - y, core),
            tp_id(x + 2, y, core),
            tp_id(x - 1, 1 - y, core),
            tp_id(x + 1, 1 - y, core),
            tp_id(x + 2, 1 - y, core),
        ]
        self.mate_slots = [self.mate] + [s + 1 - 2 * core for s in self.slots]

    def slot_of(self, kind):
        return self.slots[kind] if kind < 7 else self.mate_slots[kind - 7]

    def copy(self, piece, kind, slot, target, own=False):
        return pltpu.make_async_remote_copy(
            src_ref=self.own.at[piece] if own else self.buf.at[piece, slot],
            dst_ref=self.buf.at[piece, slot],
            send_sem=self.send.at[piece, kind],
            recv_sem=self.recv.at[piece, kind],
            device_id={"tp": target},
            device_id_type=MESH,
        )

    def start_own(self, piece):
        self.copy(piece, 0, self.me, self.right, True).start()
        self.copy(piece, 1, self.me, self.left, True).start()
        self.copy(piece, 2, self.me, self.across, True).start()
        self.copy(piece, 7, self.me, self.mate, True).start()

    def landed(self, piece, kind):
        self.copy(piece, kind, self.slot_of(kind), self.mate).wait_recv()

    def forward(self, piece, kind, as_kind, target):
        self.copy(piece, as_kind, self.slots[kind], target).start()

    def first(self, piece):
        odd = lax.rem(piece, 2)
        self.landed(piece, 0)

        @pl.when(odd == 0)
        def _():
            self.forward(piece, 0, 3, self.right)

        self.forward(piece, 0, 8, self.mate)
        self.landed(piece, 1)

        @pl.when(odd == 1)
        def _():
            self.forward(piece, 1, 3, self.left)

        self.forward(piece, 1, 9, self.mate)
        self.landed(piece, 2)
        self.forward(piece, 2, 4, self.right)
        self.forward(piece, 2, 5, self.left)
        self.forward(piece, 2, 10, self.mate)

    def second(self, piece):
        self.landed(piece, 3)
        self.forward(piece, 3, 6, self.across)
        self.forward(piece, 3, 11, self.mate)
        self.landed(piece, 4)
        self.forward(piece, 4, 12, self.mate)
        self.landed(piece, 5)
        self.forward(piece, 5, 13, self.mate)

    def third(self, piece):
        self.landed(piece, 6)
        self.forward(piece, 6, 14, self.mate)

    def mates_landed(self, piece, kinds):
        for kind in kinds:
            self.landed(piece, kind)

    def drain(self, pieces):
        def one(piece, carry):
            self.copy(piece, 0, self.me, self.right, True).wait_send()
            self.copy(piece, 1, self.me, self.left, True).wait_send()
            self.copy(piece, 2, self.me, self.across, True).wait_send()
            self.copy(piece, 7, self.me, self.mate, True).wait_send()
            for kind in (3, 4, 5, 6, 8, 9, 10, 11, 12, 13, 14):
                self.copy(piece, kind, self.me, self.mate).wait_send()
            return carry

        lax.fori_loop(0, pieces, one, 0)


def greet_tp():
    me = lax.axis_index("tp")
    barrier = pltpu.get_barrier_semaphore()

    def greet(j, carry):
        pl.semaphore_signal(barrier, inc=1, device_id={"tp": me ^ j}, device_id_type=MESH)
        return carry

    lax.fori_loop(1, TP, greet, 0)
    pl.semaphore_wait(barrier, TP - 1)


def push_copy(j, box, send, recv, incoming=False):
    me = lax.axis_index("tp")
    slot = me ^ j if incoming else me
    return pltpu.make_async_remote_copy(
        src_ref=box.at[slot],
        dst_ref=box.at[slot],
        send_sem=send.at[j],
        recv_sem=recv.at[j],
        device_id={"tp": me ^ j},
        device_id_type=MESH,
    )


def push_start(box, send, recv):
    def one(j, carry):
        push_copy(j, box, send, recv).start()
        return carry

    lax.fori_loop(1, TP, one, 0)


def push_wait(box, send, recv):
    def one(j, carry):
        push_copy(j, box, send, recv, True).wait_recv()
        return carry

    lax.fori_loop(1, TP, one, 0)

    def sent(j, carry):
        push_copy(j, box, send, recv).wait_send()
        return carry

    lax.fori_loop(1, TP, sent, 0)


def to_lanes(column):
    n = column.shape[0]
    return jnp.transpose(jnp.broadcast_to(column, (n, 128)))[0:1, :]


def to_rows(lanes):
    n = lanes.shape[1]
    return jnp.transpose(jnp.broadcast_to(lanes, (128, n)))


A_PIECES = 4
A_ROWS = ROWS // A_PIECES


def project_kernel(
    x_ref, gain_ref, wq_hbm, wk_hbm, wv_hbm, q_ref, kv_ref,
    buf, stats, wq, wk, wv, wkv, inv, accq, acckv,
    send, recv, ssend, srecv, wsend, wrecv, wsem,
):
    x, y, core = tp_coords()
    me = lax.axis_index("tp")
    load_q = pltpu.make_async_copy(wq_hbm, wq, wsem.at[0])
    load_k = pltpu.make_async_copy(wk_hbm, wk, wsem.at[1])
    load_v = pltpu.make_async_copy(wv_hbm, wv, wsem.at[2])
    load_k.start()
    load_v.start()
    load_q.start()

    for piece in range(A_PIECES):
        rows = x_ref[piece].astype(F32)
        total = jnp.sum(rows * rows, axis=1, keepdims=True)
        stats[me, 0:1, piece * A_ROWS : (piece + 1) * A_ROWS] = to_lanes(total)
    stats[me, 1:2, :] = gain_ref[...].astype(F32)

    greet_tp()
    gather = Gather(x_ref, buf, send, recv)
    push_start(stats, ssend, srecv)
    gather.start_own(0)
    gather.start_own(1)

    load_k.wait()
    load_v.wait()

    def join(i, carry):
        at = pl.ds(pl.multiple_of(i * WIDTH, WIDTH), WIDTH)
        wkv[core, at, :] = jnp.concatenate([wk[at, :], wv[at, :]], axis=1)
        return carry

    lax.fori_loop(0, D // WIDTH, join, 0)

    push_wait(stats, ssend, srecv)
    share = pltpu.make_async_remote_copy(
        src_ref=wkv.at[core],
        dst_ref=wkv.at[core],
        send_sem=wsend,
        recv_sem=wrecv,
        device_id={"tp": gather.mate},
        device_id_type=MESH,
    )
    share_in = pltpu.make_async_remote_copy(
        src_ref=wkv.at[1 - core],
        dst_ref=wkv.at[1 - core],
        send_sem=wsend,
        recv_sem=wrecv,
        device_id={"tp": gather.mate},
        device_id_type=MESH,
    )
    share.start()
    squares = stats[0, 0:1, :]
    for slot in range(1, TP):
        squares = squares + stats[slot, 0:1, :]
    scale = lax.rsqrt(squares / D + EPS_IN)
    for piece in range(A_PIECES):
        inv[piece] = to_rows(scale[:, piece * A_ROWS : (piece + 1) * A_ROWS])
    accq[...] = jnp.zeros_like(accq)
    acckv[...] = jnp.zeros_like(acckv)
    load_q.wait()
    share_in.wait_recv()

    def consume(piece, slot, own=False):
        at = pl.ds(pl.multiple_of(slot * WIDTH, WIDTH), WIDTH)
        gain = stats[slot, 1:2, :]
        parts = []
        for g in range(WIDTH // 128):
            lanes = slice(g * 128, (g + 1) * 128)
            values = (x_ref[piece, :, lanes] if own else buf[piece, slot, :, lanes]).astype(F32)
            values = values * inv[piece] * gain[:, lanes]
            limit = CLIP_RATIO * jnp.max(jnp.abs(values), axis=-1, keepdims=True)
            parts.append(jnp.clip(values, -limit, limit).astype(BF16))
        quantized = jnp.concatenate(parts, axis=1)
        accq[piece] += jnp.dot(quantized, wq[at, :], preferred_element_type=F32)

        @pl.when(lax.rem(piece, 2) == core)
        def _():
            both = jnp.concatenate([wkv[0, at, :], wkv[1, at, :]], axis=1)
            acckv[piece // 2] += jnp.dot(quantized, both, preferred_element_type=F32)

    def pick(options, i):
        value = options[0]
        for n, option in enumerate(options[1:]):
            value = jnp.where(i == n + 1, option, value)
        return value

    def consume_all(piece, slots):
        def one(i, carry):
            consume(piece, pick(slots, i))
            return carry

        lax.fori_loop(0, len(slots), one, 0)

    group1 = gather.slots[:3] + gather.mate_slots[:4]
    group2 = gather.slots[3:6] + gather.mate_slots[4:7]
    group3 = gather.slots[6:7] + gather.mate_slots[7:8]

    def step(t, carry):
        @pl.when(t < A_PIECES)
        def _():
            consume(t, me, True)
            gather.first(t)

        @pl.when(t + 2 < A_PIECES)
        def _():
            gather.start_own(t + 2)

        @pl.when((t >= 1) & (t <= A_PIECES))
        def _():
            gather.second(t - 1)

        @pl.when((t >= 2) & (t <= A_PIECES + 1))
        def _():
            gather.third(t - 2)

        @pl.when(t < A_PIECES)
        def _():
            gather.mates_landed(t, (7, 8, 9, 10))
            consume_all(t, group1)

        @pl.when((t >= 1) & (t <= A_PIECES))
        def _():
            gather.mates_landed(t - 1, (11, 12, 13))
            consume_all(t - 1, group2)

        @pl.when((t >= 2) & (t <= A_PIECES + 1))
        def _():
            gather.mates_landed(t - 2, (14,))
            consume_all(t - 2, group3)

        return carry

    lax.fori_loop(0, A_PIECES + 2, step, 0)
    for piece in range(A_PIECES):
        for head in range(2):
            q_ref[head, piece] = accq[piece, :, head * HD : (head + 1) * HD].astype(BF16)
    for part in range(2):
        done = acckv[part].astype(BF16)
        at = slice(part * A_ROWS, (part + 1) * A_ROWS)
        kv_ref[at, :] = jnp.concatenate(
            [done[:, 0:64], done[:, 128:192], done[:, 64:128], done[:, 192:256]], axis=1
        )
    share.wait_send()
    gather.drain(A_PIECES)


def project(x, gain, w_query, w_key, w_value):
    any_space = pl.BlockSpec(memory_space=pl.ANY)
    vmem = pl.BlockSpec(memory_space=pltpu.VMEM)
    dma = pltpu.SemaphoreType.DMA
    return pl.pallas_call(
        project_kernel,
        out_shape=(
            jax.ShapeDtypeStruct((2, A_PIECES, A_ROWS, HD), BF16),
            jax.ShapeDtypeStruct((2 * A_ROWS, 2 * HD), BF16),
        ),
        in_specs=[vmem, vmem, any_space, any_space, any_space],
        out_specs=(vmem, vmem),
        scratch_shapes=[
            pltpu.VMEM((A_PIECES, TP, A_ROWS, WIDTH), BF16),
            pltpu.VMEM((TP, 2, WIDTH), F32),
            pltpu.VMEM((D, 256), BF16),
            pltpu.VMEM((D, 64), BF16),
            pltpu.VMEM((D, 64), BF16),
            pltpu.VMEM((2, D, 128), BF16),
            pltpu.VMEM((A_PIECES, A_ROWS, 128), F32),
            pltpu.VMEM((A_PIECES, A_ROWS, 256), F32),
            pltpu.VMEM((2, A_ROWS, 256), F32),
            dma((A_PIECES, 15)),
            dma((A_PIECES, 15)),
            dma((TP,)),
            dma((TP,)),
            dma,
            dma,
            dma((3,)),
        ],
        compiler_params=pltpu.CompilerParams(
            collective_id=0, has_side_effects=True, vmem_limit_bytes=VMEM_LIMIT
        ),
        name="project",
    )(x.reshape(A_PIECES, A_ROWS, WIDTH), gain.reshape(1, WIDTH), w_query, w_key, w_value)


KEYS = 2 * A_ROWS
QROWS = 2 * ROWS
QCHUNK = 256


def attend_kernel(q_ref, kv_ref, sign_ref, out_ref, buf, top, total, acc, send, recv):
    ctx = lax.axis_index("ctx")
    core = lax.rem(lax.axis_index("tp"), 2)
    mate = lax.axis_index("tp") + 1 - 2 * core
    row, z = ctx // 8, lax.rem(ctx, 8)
    sense = 1 - 2 * core
    other = (1 - row) * 8 + z

    def along(r, delta):
        return r * 8 + lax.rem(z + delta + 16, 8)

    ahead, behind = along(row, sense), along(row, -sense)

    def copy(kind, block, half, target, own=False):
        return pltpu.make_async_remote_copy(
            src_ref=kv_ref if own else buf.at[block, half],
            dst_ref=buf.at[block, half],
            send_sem=send.at[kind],
            recv_sem=recv.at[kind],
            device_id=target,
            device_id_type=MESH,
        )

    to_mate, to_ahead, to_behind = {"tp": mate}, {"ctx": ahead}, {"ctx": behind}
    barrier = pltpu.get_barrier_semaphore()
    for target in (to_mate, to_ahead, to_behind, {"ctx": other}):
        pl.semaphore_signal(barrier, inc=1, device_id=target, device_id_type=MESH)
    pl.semaphore_wait(barrier, 4)

    copy(1, ctx, core, to_ahead, True).start()
    copy(9, ctx, core, to_behind, True).start()
    copy(0, ctx, core, {"ctx": other}, True).start()
    copy(15, ctx, core, to_mate, True).start()

    top[...] = jnp.full_like(top, FAR_BELOW)
    total[...] = jnp.zeros_like(total)
    acc[...] = jnp.zeros_like(acc)
    factor = HD ** (-0.5) * LOG2E

    def unit(keys, values, half, masked):
        for chunk in range(QROWS // QCHUNK):
            at = slice(chunk * QCHUNK, (chunk + 1) * QCHUNK)
            scores = lax.dot_general(
                q_ref[at, :], keys, (((1,), (1,)), ((), ())), preferred_element_type=F32
            )
            if masked:
                base = (chunk * QCHUNK) % ROWS
                q_pos = base + lax.broadcasted_iota(jnp.int32, (QCHUNK, KEYS), 0)
                k_row = lax.broadcasted_iota(jnp.int32, (QCHUNK, KEYS), 1)
                k_pos = (k_row // A_ROWS) * (2 * A_ROWS) + half * A_ROWS + lax.rem(k_row, A_ROWS)
                seen = k_pos <= q_pos
                scores = jnp.where(seen, scores, FAR_BELOW)
            high = jnp.max(scores, axis=-1, keepdims=True)
            before = top[at, :]
            now = jnp.maximum(before, jnp.broadcast_to(high, (QCHUNK, 128)))
            decay = jnp.exp2((before - now) * factor)
            shift = now * factor
            left = jnp.exp2(scores[:, :128] * factor - shift)
            right = jnp.exp2(scores[:, 128:] * factor - shift)
            if masked:
                left = jnp.where(seen[:, :128], left, 0.0)
                right = jnp.where(seen[:, 128:], right, 0.0)
            total[at, :] = decay * total[at, :] + (left + right)
            weights = jnp.concatenate([left.astype(BF16), right.astype(BF16)], axis=1)
            mixed = jnp.dot(weights, values, preferred_element_type=F32)
            acc[at, :] = decay * acc[at, :] + mixed
            top[at, :] = now

    unit(kv_ref[:, :HD], kv_ref[:, HD:], core, True)

    def landed(kind, block, half):
        copy(kind, block, half, to_mate).wait_recv()

    def earlier(block, half):
        @pl.when(block < ctx)
        def _():
            unit(buf[block, half, :, :HD], buf[block, half, :, HD:], half, False)

    landed(15, ctx, 1 - core)
    unit(buf[ctx, 1 - core, :, :HD], buf[ctx, 1 - core, :, HD:], 1 - core, True)

    def step(n, carry):
        d, r = n // 2 + 1, lax.rem(n, 2)
        its_row = jnp.where(r == 0, row, 1 - row)

        @pl.when(n == 1)
        def _():
            landed(0, other, core)
            copy(2, other, core, to_ahead).start()
            copy(10, other, core, to_behind).start()
            copy(16, other, core, to_mate).start()

        @pl.when(n < 8)
        def _():
            block = along(its_row, -sense * d)
            landed(1 + n, block, core)

            @pl.when(n < 6)
            def _():
                copy(3 + n, block, core, to_ahead).start()

            copy(17 + n, block, core, to_mate).start()

        @pl.when(n < 6)
        def _():
            block = along(its_row, sense * d)
            landed(9 + n, block, core)

            @pl.when(n < 4)
            def _():
                copy(11 + n, block, core, to_behind).start()

            copy(25 + n, block, core, to_mate).start()

        def one(u, carry):
            late = u // 2
            back = lax.rem(u, 2)
            m = n - late
            half = jnp.where(late == 1, 1 - core, core)
            its = jnp.where(lax.rem(m + 2, 2) == 0, row, 1 - row)
            dist = (m + 2) // 2
            flip = jnp.where(late == 1, -sense, sense)
            delta = jnp.where(back == 0, -flip, flip) * dist
            block = along(its, delta)
            valid = (m >= 0) & (m < jnp.where(back == 0, 8, 6))

            @pl.when(valid)
            def _():
                @pl.when(late == 1)
                def _():
                    landed(jnp.where(back == 0, 17, 25) + m, block, 1 - core)

                earlier(block, half)

            return carry

        lax.fori_loop(0, 4, one, 0)

        @pl.when(n == 1)
        def _():
            earlier(other, core)

        @pl.when(n == 2)
        def _():
            landed(16, other, 1 - core)
            earlier(other, 1 - core)

        return carry

    lax.fori_loop(0, 9, step, 0)

    for head in range(2):
        signs = (2 * sign_ref[head : head + 1, :] - 1).astype(F32)
        for chunk in range(ROWS // QCHUNK):
            at = slice(head * ROWS + chunk * QCHUNK, head * ROWS + (chunk + 1) * QCHUNK)
            whole = jnp.sum(total[at, :], axis=-1, keepdims=True)
            attended = (acc[at, :] / whole).astype(BF16)
            out_ref[chunk * QCHUNK : (chunk + 1) * QCHUNK, head * HD : (head + 1) * HD] = (
                attended.astype(F32) * signs
            ).astype(BF16)

    def drain(kind, carry):
        copy(kind, ctx, core, to_mate).wait_send()
        return carry

    lax.fori_loop(0, 31, drain, 0)


def attend(q, kv, sign_bits):
    vmem = pl.BlockSpec(memory_space=pltpu.VMEM)
    dma = pltpu.SemaphoreType.DMA
    return pl.pallas_call(
        attend_kernel,
        out_shape=jax.ShapeDtypeStruct((ROWS, 2 * HD), BF16),
        in_specs=[vmem, vmem, vmem],
        out_specs=vmem,
        scratch_shapes=[
            pltpu.VMEM((16, 2, KEYS, 2 * HD), BF16),
            pltpu.VMEM((QROWS, 128), F32),
            pltpu.VMEM((QROWS, 128), F32),
            pltpu.VMEM((QROWS, HD), F32),
            dma((31,)),
            dma((31,)),
        ],
        compiler_params=pltpu.CompilerParams(
            collective_id=1, has_side_effects=True, vmem_limit_bytes=VMEM_LIMIT
        ),
        name="attend",
    )(q.reshape(QROWS, HD), kv, sign_bits)


C_PIECES = 4
C_ROWS = ROWS // C_PIECES
C_WIDTH = 2 * HD
STRIP = 16


def output_kernel(
    s_ref, w_hbm, teacher_ref, out_ref, loss_ref,
    buf, w, rotated, branch, box1, box2,
    send, recv, send1, recv1, send2, recv2, wsem,
):
    me = lax.axis_index("tp")
    load = pltpu.make_async_copy(w_hbm, w, wsem)
    load.start()
    greet_tp()
    gather = Gather(s_ref, buf, send, recv)
    gather.start_own(0)
    gather.start_own(1)
    load.wait()

    def consume(piece):
        def strip(i, carry):
            at = pl.ds(pl.multiple_of(i * STRIP, STRIP), STRIP)
            heads = []
            for slot in range(TP):
                both = buf[piece, slot, at, :].astype(F32)
                heads += [both[:, :HD], both[:, HD:]]
            span = 1
            while span < QH:
                for h in range(QH):
                    if not h & span:
                        a, b = heads[h], heads[h + span]
                        heads[h], heads[h + span] = a + b, a - b
                span *= 2
            for h in range(QH):
                value = heads[h] * QH ** (-0.5)
                limit = CLIP_RATIO * jnp.max(jnp.abs(value), axis=-1, keepdims=True)
                rotated[at, h * HD : (h + 1) * HD] = jnp.clip(value, -limit, limit).astype(BF16)
            return carry

        lax.fori_loop(0, C_ROWS // STRIP, strip, 0)
        branch[piece] = jnp.dot(rotated[...], w[...], preferred_element_type=F32)

    def step(t, carry):
        @pl.when(t < C_PIECES)
        def _():
            here = pltpu.make_async_copy(s_ref.at[t], buf.at[t, me], wsem)
            here.start()
            gather.first(t)
            here.wait()

        @pl.when(t + 2 < C_PIECES)
        def _():
            gather.start_own(t + 2)

        @pl.when((t >= 1) & (t <= C_PIECES))
        def _():
            gather.second(t - 1)

        @pl.when((t >= 2) & (t <= C_PIECES + 1))
        def _():
            gather.third(t - 2)
            gather.mates_landed(t - 2, range(7, 15))
            consume(t - 2)

        return carry

    lax.fori_loop(0, C_PIECES + 2, step, 0)

    for piece in range(C_PIECES):
        rows = branch[piece]
        total = jnp.sum(rows * rows, axis=1, keepdims=True)
        box1[me, 0:1, piece * C_ROWS : (piece + 1) * C_ROWS] = to_lanes(total)
    push_start(box1, send1, recv1)
    gather.drain(C_PIECES)
    push_wait(box1, send1, recv1)
    squares = box1[0, 0:1, :]
    for slot in range(1, TP):
        squares = squares + box1[slot, 0:1, :]
    inverse = lax.rsqrt(squares / D + EPS_OUT)
    for piece in range(C_PIECES):
        scale = to_rows(inverse[:, piece * C_ROWS : (piece + 1) * C_ROWS])
        partial = jnp.zeros((C_ROWS, 128), F32)
        for g in range(WIDTH // 128):
            lanes = slice(g * 128, (g + 1) * 128)
            normal = branch[piece, :, lanes] * scale
            out_ref[piece, :, lanes] = normal.astype(BF16)
            difference = normal - teacher_ref[piece, :, lanes].astype(F32)
            partial = partial + difference * difference
        total = jnp.sum(partial, axis=1, keepdims=True)
        box2[me, 0:1, piece * C_ROWS : (piece + 1) * C_ROWS] = to_lanes(total)
    push_start(box2, send2, recv2)
    push_wait(box2, send2, recv2)
    loss = box2[0, 0:1, :]
    for slot in range(1, TP):
        loss = loss + box2[slot, 0:1, :]
    loss_ref[...] = loss / D


def output(signed, w_out, teacher):
    any_space = pl.BlockSpec(memory_space=pl.ANY)
    vmem = pl.BlockSpec(memory_space=pltpu.VMEM)
    dma = pltpu.SemaphoreType.DMA
    student, loss = pl.pallas_call(
        output_kernel,
        out_shape=(
            jax.ShapeDtypeStruct((C_PIECES, C_ROWS, WIDTH), BF16),
            jax.ShapeDtypeStruct((1, ROWS), F32),
        ),
        in_specs=[vmem, any_space, vmem],
        out_specs=(vmem, vmem),
        scratch_shapes=[
            pltpu.VMEM((C_PIECES, TP, C_ROWS, C_WIDTH), BF16),
            pltpu.VMEM((QH * HD, WIDTH), BF16),
            pltpu.VMEM((C_ROWS, QH * HD), BF16),
            pltpu.VMEM((C_PIECES, C_ROWS, WIDTH), F32),
            pltpu.VMEM((TP, 1, ROWS), F32),
            pltpu.VMEM((TP, 1, ROWS), F32),
            dma((C_PIECES, 15)),
            dma((C_PIECES, 15)),
            dma((TP,)),
            dma((TP,)),
            dma((TP,)),
            dma((TP,)),
            dma,
        ],
        compiler_params=pltpu.CompilerParams(
            collective_id=2, has_side_effects=True, vmem_limit_bytes=VMEM_LIMIT
        ),
        name="output",
    )(
        signed.reshape(C_PIECES, C_ROWS, C_WIDTH),
        w_out,
        teacher.reshape(C_PIECES, C_ROWS, WIDTH),
    )
    return student.reshape(ROWS, WIDTH), loss.reshape(ROWS)


def body(hidden_in, norm_gain, w_query, w_key, w_value, sign_bits, w_out, teacher):
    q, kv = project(hidden_in, norm_gain, w_query, w_key, w_value)
    signed = attend(q, kv, sign_bits)
    return output(signed, w_out, teacher)


def solution(mesh):
    in_specs = (
        P("ctx", "tp"),
        P("tp"),
        P(None, "tp"),
        P(None, "tp"),
        P(None, "tp"),
        P("tp", None),
        P(None, "tp"),
        P("ctx", "tp"),
    )
    out_specs = (P("ctx", "tp"), P("ctx"))
    return jax.shard_map(body, mesh=mesh, in_specs=in_specs, out_specs=out_specs, check_vma=False)
```

time: 549 us -> 146 us (0.27); the launches traced: 540 us -> 145 us
  waiting for transfers between devices: 220 us -> 0 us
  Pallas kernels: 0 us -> 135 us
  matrix products: 91.8 us -> 0 us
  other arithmetic: 86.2 us -> 0 us
  blocking collectives: 75.9 us -> 0 us
  local copies, waits for them, and re-layouts: 39.5 us -> 9.85 us
  between operations: 14.2 us -> 0.66 us
  starting transfers between devices: 11.7 us -> 0 us
    all_gather x4 -> x0, waiting for transfers between devices: 217 us -> none  [the longest x1 83.8 us: body(): block_keys = lax.all_gather(key_vals[0], 'ctx', axis=0, tiled=True)]
    pallas_call x0 -> x3, Pallas kernels: none -> 135 us  [the longest x1 51.3 us: project(): pl.pallas_call(project_kernel, out_shape=(jax.ShapeDtypeStruct((2, A_PIEC...]
    dot_general x37 -> x0, matrix products: 91.8 us -> none  [the longest x16 44.5 us: advance(): jnp.einsum('kgqn,nkd->kgqd', weights.astype(jnp.bfloat16), values_now, pr...]
    psum x2 -> x0, blocking collectives: 55.8 us -> none  [the longest x1 29 us: body(): row_loss = lax.psum(jnp.sum(difference * difference, axis=-1), 'tp') / D]
    convert_element_type x4 -> x0, other arithmetic: 44.7 us -> none  [the longest x1 35.1 us: body(): quantized = clip_groups(normed).astype(jnp.bfloat16)]
    all_gather x1 -> x0, blocking collectives: 20.1 us -> none  [body(): lax.all_gather(norm_gain, 'tp', axis=0, tiled=True)]
    reduce_sum x18 -> x0, other arithmetic: 14.3 us -> none  [the longest x16 9.01 us: advance(): weight_sum = decay * weight_sum + jnp.sum(weights, axis=-1)]
    unnamed x5 -> x0, other arithmetic: 12.1 us -> none
  transfers between devices with their start and end apart: 6 -> 0, of which waited for: 6 -> 0; matrix products, arithmetic and copies ran while one was open for 3% -> 0% of each run, Pallas kernels for 0% -> 0%
where the time goes in v1:
time: 146 us; the launch traced here: 145 us
  Pallas kernels  135 us (92%)
  local copies, waits for them, and re-layouts  9.85 us (7%)
    pallas_call x1, Pallas kernels, project(): pl.pallas_call(project_kernel, out_shape=(jax.ShapeDtypeStruct((2, A_PIEC...  51.3 us
    pallas_call x1, Pallas kernels, attend(): pl.pallas_call(attend_kernel, out_shape=jax.ShapeDtypeStruct((ROWS, 2 * H...  42.5 us
    pallas_call x1, Pallas kernels, output(): pl.pallas_call(output_kernel, out_shape=(jax.ShapeDtypeStruct((C_PIECES,...  40.7 us
    unnamed x4, local copies, waits for them, and re-layouts  8.59 us

profile of v1, /device:TPU:17, one launch (start us, length us, event | category | flops | bytes accessed | tf_op | source)
XLA Modules:
  0.0 145.1 jit_solution(13324593515130875886)
XLA Ops:
  0.6 1.3 reshape.26.gain_ref
  1.9 2.8 %copy.10.wk_hbm = bf16[8192,64]{1,0:T(8,128)(2,1)} copy(bf16[8192,64]{0,1:T(8,128)(2,1)} %param.11) | data formatting | bytes 2097152 | tf_op args[3]
  4.7 2.7 %copy.11.wv_hbm = bf16[8192,64]{1,0:T(8,128)(2,1)} copy(bf16[8192,64]{0,1:T(8,128)(2,1)} %param.12) | data formatting | bytes 2097152 | tf_op args[4]
  7.4 51.3 %project.1 = (bf16[2,4,128,128]{3,2,1,0:T(8,128)(2,1)}, bf16[256,256]{1,0:T(8,128)(2,1)}) custom-call(bf16[4,128,512]{2,1,0:T(8,128)(2,1)} %bitcast.7, bf16[1,512]{1,0:T(2,128)(2,1)} %reshape.26.gain_ref, bf16[8192,256]{1,0:T(8,128)(2,1)} %wq_hbm.1, bf16[8192,64]{1,0:T(8,128)(2,1)} %copy.10.wk_hbm, bf16[8192,64]{1,0:T(8,128)(2,1)} %copy.11.wv_hbm), custom_call_target="tpu_custom_call" | custom-call | tf_op jit(solution)/shard_map/project/pallas_call | solution.py:346
  58.7 42.5 %attend.1 = bf16[512,256]{1,0:T(8,128)(2,1)} custom-call(bf16[1024,128]{1,0:T(8,128)(2,1)} %bitcast.10, bf16[256,256]{1,0:T(8,128)(2,1)} %get-tuple-element.7.kv_ref, s32[2,128]{1,0:T(2,128)} %sign_ref.1), custom_call_target="tpu_custom_call" | custom-call | tf_op jit(solution)/shard_map/attend/pallas_call | solution.py:555
  101.3 40.7 %output.1 = (bf16[4,128,512]{2,1,0:T(8,128)(2,1)}, f32[1,512]{1,0:T(1,128)}) custom-call(bf16[4,128,256]{2,1,0:T(8,128)(2,1)} %bitcast.6, bf16[4096,512]{1,0:T(8,128)(2,1)} %w_hbm.1, bf16[4,128,512]{2,1,0:T(8,128)(2,1)} %bitcast.8), custom_call_target="tpu_custom_call" | custom-call | tf_op jit(solution)/shard_map/output/pallas_call | solution.py:678
  142.0 1.9 %copy.14 = bf16[512,512]{1,0:T(8,128)(2,1)} copy(bf16[512,512]{1,0:T(8,128)(2,1)} %bitcast.9) | data formatting | bytes 1048576
  143.9 1.2 copy.15

commit v2 on v0

v2 whole, which is shorter than its diff:
```python
import functools

import jax
import jax.numpy as jnp
from jax import lax
from jax.experimental import pallas as pl
from jax.experimental.pallas import tpu as pltpu
from jax.sharding import PartitionSpec as P

MESH = pl.DeviceIdType.MESH
F32 = jnp.float32
BF16 = jnp.bfloat16

D = 8192
QH = 32
HD = 128
ROWS = 512
TP = 16
WIDTH = D // TP
EPS_IN = 1e-05
EPS_OUT = 1e-06
CLIP_RATIO = 0.9
FAR_BELOW = -1e30
LOG2E = 1.4426950408889634
VMEM_LIMIT = 62 * 1024 * 1024


def tp_id(x, y, core):
    return lax.rem(x + 8, 4) * 4 + y * 2 + core


def tp_coords():
    me = lax.axis_index("tp")
    return me // 4, lax.rem(me // 2, 2), lax.rem(me, 2)


class Gather:
    def __init__(self, buf, send, recv):
        self.buf, self.send, self.recv = buf, send, recv
        x, y, core = tp_coords()
        self.core = core
        self.me = tp_id(x, y, core)
        self.right, self.left = tp_id(x + 1, y, core), tp_id(x - 1, y, core)
        self.across, self.mate = tp_id(x, 1 - y, core), tp_id(x, y, 1 - core)
        self.slots = [
            tp_id(x - 1, y, core),
            tp_id(x + 1, y, core),
            tp_id(x, 1 - y, core),
            tp_id(x + 2, y, core),
            tp_id(x - 1, 1 - y, core),
            tp_id(x + 1, 1 - y, core),
            tp_id(x + 2, 1 - y, core),
        ]
        self.mate_slots = [self.mate] + [s + 1 - 2 * core for s in self.slots]

    def slot_of(self, kind):
        return self.slots[kind] if kind < 7 else self.mate_slots[kind - 7]

    def copy(self, piece, kind, slot, target):
        return pltpu.make_async_remote_copy(
            src_ref=self.buf.at[piece, slot],
            dst_ref=self.buf.at[piece, slot],
            send_sem=self.send.at[piece, kind],
            recv_sem=self.recv.at[piece, kind],
            device_id={"tp": target},
            device_id_type=MESH,
        )

    def start_sideways(self, piece):
        self.copy(piece, 0, self.me, self.right).start()
        self.copy(piece, 1, self.me, self.left).start()

    def start_near(self, piece):
        self.copy(piece, 2, self.me, self.across).start()
        self.copy(piece, 7, self.me, self.mate).start()

    def landed(self, piece, kind):
        self.copy(piece, kind, self.slot_of(kind), self.mate).wait_recv()

    def forward(self, piece, kind, as_kind, target):
        self.copy(piece, as_kind, self.slots[kind], target).start()

    def from_sides(self, piece):
        self.landed(piece, 0)
        if piece % 2 == 0:
            self.forward(piece, 0, 3, self.right)
        self.forward(piece, 0, 8, self.mate)
        self.landed(piece, 1)
        if piece % 2 == 1:
            self.forward(piece, 1, 3, self.left)
        self.forward(piece, 1, 9, self.mate)

    def from_across(self, piece):
        self.landed(piece, 2)
        self.forward(piece, 2, 4, self.right)
        self.forward(piece, 2, 5, self.left)
        self.forward(piece, 2, 10, self.mate)

    def from_far(self, piece):
        self.landed(piece, 3)
        self.forward(piece, 3, 6, self.across)
        self.forward(piece, 3, 11, self.mate)

    def from_diagonal(self, piece):
        self.landed(piece, 4)
        self.forward(piece, 4, 12, self.mate)
        self.landed(piece, 5)
        self.forward(piece, 5, 13, self.mate)

    def from_far_across(self, piece):
        self.landed(piece, 6)
        self.forward(piece, 6, 14, self.mate)

    def mates_landed(self, piece, kinds):
        for kind in kinds:
            self.landed(piece, kind)

    def drain(self, pieces):
        def one(piece, carry):
            for kind in range(15):
                self.copy(piece, kind, self.me, self.mate).wait_send()
            return carry

        lax.fori_loop(0, pieces, one, 0)


def push_copy(j, box, send, recv, incoming=False):
    me = lax.axis_index("tp")
    slot = me ^ j if incoming else me
    return pltpu.make_async_remote_copy(
        src_ref=box.at[slot],
        dst_ref=box.at[slot],
        send_sem=send.at[j],
        recv_sem=recv.at[j],
        device_id={"tp": me ^ j},
        device_id_type=MESH,
    )


def push_start(box, send, recv):
    def one(j, carry):
        push_copy(j, box, send, recv).start()
        return carry

    lax.fori_loop(1, TP, one, 0)


def push_wait(box, send, recv):
    def one(j, carry):
        push_copy(j, box, send, recv, True).wait_recv()
        return carry

    lax.fori_loop(1, TP, one, 0)

    def sent(j, carry):
        push_copy(j, box, send, recv).wait_send()
        return carry

    lax.fori_loop(1, TP, sent, 0)


def to_lanes(column):
    n = column.shape[0]
    return jnp.transpose(jnp.broadcast_to(column, (n, 128)))[0:1, :]


def to_rows(lanes):
    n = lanes.shape[1]
    return jnp.transpose(jnp.broadcast_to(lanes, (128, n)))


PIECES = 4
PROWS = ROWS // PIECES
QROWS = 2 * ROWS
HALF = ROWS // 2
STRIP = 16


def pick(options, i):
    value = options[0]
    for n, option in enumerate(options[1:]):
        value = jnp.where(i == n + 1, option, value)
    return value


def block_kernel(
    x_hbm, gain_ref, wq_hbm, wk_hbm, wv_hbm, sign_ref, wo_hbm, teacher_hbm,
    student_hbm, loss_ref,
    xraw, xbuf, stats, wq, wkv, accq, acckv, q, kvbuf, top, total, acc,
    sbuf, wo, rotated, branch, teacher, student, box1, box2,
    xsend, xrecv, ksend, krecv, ssend, srecv,
    psend0, precv0, psend1, precv1, psend2, precv2, wsend, wrecv, load_sem, x_sem,
):
    me = lax.axis_index("tp")
    ctx = lax.axis_index("ctx")
    rows = Gather(xbuf, xsend, xrecv)
    core, mate = rows.core, rows.mate

    x_loads = [
        pltpu.make_async_copy(x_hbm.at[p], xraw.at[p], x_sem.at[p]) for p in range(PIECES)
    ]
    for load in x_loads:
        load.start()

    def half(base, whose):
        return pl.ds(pl.multiple_of(base + whose * 64, 64), 64)

    load_k = pltpu.make_async_copy(wk_hbm, wkv.at[half(0, core)], load_sem.at[0])
    load_v = pltpu.make_async_copy(wv_hbm, wkv.at[half(128, core)], load_sem.at[1])
    load_q = pltpu.make_async_copy(wq_hbm, wq, load_sem.at[2])
    load_o = pltpu.make_async_copy(wo_hbm, wo, load_sem.at[3])
    load_t = pltpu.make_async_copy(teacher_hbm, teacher, load_sem.at[4])
    load_k.start()
    load_v.start()
    load_q.start()

    row, z = ctx // 8, lax.rem(ctx, 8)
    sense = 1 - 2 * core
    other = (1 - row) * 8 + z

    def along(r, delta):
        return r * 8 + lax.rem(z + delta + 16, 8)

    to_ahead, to_behind = {"ctx": along(row, sense)}, {"ctx": along(row, -sense)}
    to_other, to_mate = {"ctx": other}, {"tp": mate}

    barrier = pltpu.get_barrier_semaphore()

    def greet(j, carry):
        pl.semaphore_signal(barrier, inc=1, device_id={"tp": me ^ j}, device_id_type=MESH)
        return carry

    lax.fori_loop(1, TP, greet, 0)
    for target in (to_ahead, to_behind, to_other):
        pl.semaphore_signal(barrier, inc=1, device_id=target, device_id_type=MESH)

    for p in range(PIECES):
        x_loads[p].wait()
        values = xraw[p].astype(F32)
        stats[me, 0:1, p * PROWS : (p + 1) * PROWS] = to_lanes(
            jnp.sum(values * values, axis=1, keepdims=True)
        )
    pl.semaphore_wait(barrier, TP - 1 + 3)

    push_start(stats, psend0, precv0)
    load_o.start()
    load_t.start()
    load_k.wait()
    load_v.wait()

    def share(base, whose, n):
        return pltpu.make_async_remote_copy(
            src_ref=wkv.at[half(base, whose)],
            dst_ref=wkv.at[half(base, whose)],
            send_sem=wsend.at[n],
            recv_sem=wrecv.at[n],
            device_id=to_mate,
            device_id_type=MESH,
        )

    share(0, core, 0).start()
    share(128, core, 1).start()
    push_wait(stats, psend0, precv0)
    squares = stats[0, 0:1, :]
    for slot in range(1, TP):
        squares = squares + stats[slot, 0:1, :]
    scale = lax.rsqrt(squares / D + EPS_IN)
    gain = gain_ref[...].astype(F32).reshape(1, WIDTH)
    for p in range(PIECES):
        by_row = to_rows(scale[:, p * PROWS : (p + 1) * PROWS])
        for g in range(WIDTH // 128):
            lanes = slice(g * 128, (g + 1) * 128)
            values = xraw[p, :, lanes].astype(F32) * by_row * gain[:, lanes]
            limit = CLIP_RATIO * jnp.max(jnp.abs(values), axis=-1, keepdims=True)
            xbuf[p, me, :, lanes] = jnp.clip(values, -limit, limit).astype(BF16)
    accq[...] = jnp.zeros_like(accq)
    acckv[...] = jnp.zeros_like(acckv)

    for p in range(PIECES):
        rows.start_sideways(p)
        rows.start_near(p)
    load_q.wait()
    share(0, 1 - core, 0).wait_recv()
    share(128, 1 - core, 1).wait_recv()

    def consume(part, chip):
        at = pl.ds(pl.multiple_of(chip * 2 * WIDTH, 2 * WIDTH), 2 * WIDTH)
        both = [
            jnp.concatenate([xbuf[2 * part, slot], xbuf[2 * part + 1, slot]], axis=0)
            for slot in (2 * chip, 2 * chip + 1)
        ]
        quantized = jnp.concatenate(both, axis=1)
        accq[part] += jnp.dot(quantized, wq[at, :], preferred_element_type=F32)

        @pl.when(core == part)
        def _():
            acckv[...] += lax.dot_general(
                quantized, wkv[:, at], (((1,), (1,)), ((), ())), preferred_element_type=F32
            )

    def consume_all(part, kinds):
        chips = []
        for kind in kinds:
            for p in (2 * part, 2 * part + 1):
                rows.landed(p, 7 if kind is None else 8 + kind)
            chips.append((me if kind is None else rows.slots[kind]) // 2)

        def one(i, carry):
            consume(part, pick(chips, i))
            return carry

        lax.fori_loop(0, len(chips), one, 0)

    def kcopy(kind, block, part, target):
        return pltpu.make_async_remote_copy(
            src_ref=kvbuf.at[block, part],
            dst_ref=kvbuf.at[block, part],
            send_sem=ksend.at[kind],
            recv_sem=krecv.at[kind],
            device_id=target,
            device_id_type=MESH,
        )

    def klanded(kind, block, part):
        kcopy(kind, block, part, to_mate).wait_recv()

    def start_ring():
        kcopy(1, ctx, core, to_ahead).start()
        kcopy(9, ctx, core, to_behind).start()
        kcopy(0, ctx, core, to_other).start()
        kcopy(15, ctx, core, to_mate).start()

    def hop(n):
        d = n // 2 + 1
        its_row = jnp.where(lax.rem(n, 2) == 0, row, 1 - row)

        @pl.when(n == 1)
        def _():
            klanded(0, other, core)
            kcopy(2, other, core, to_ahead).start()
            kcopy(10, other, core, to_behind).start()
            kcopy(16, other, core, to_mate).start()

        back = along(its_row, -sense * d)
        klanded(1 + n, back, core)

        @pl.when(n < 6)
        def _():
            kcopy(3 + n, back, core, to_ahead).start()

        kcopy(17 + n, back, core, to_mate).start()

        @pl.when(n < 6)
        def _():
            front = along(its_row, sense * d)
            klanded(9 + n, front, core)

            @pl.when(n < 4)
            def _():
                kcopy(11 + n, front, core, to_behind).start()

            kcopy(25 + n, front, core, to_mate).start()

    rows.from_sides(0)
    rows.from_sides(1)
    rows.from_across(0)
    consume_all(0, (None,))
    rows.from_sides(2)
    rows.from_sides(3)
    rows.from_across(1)
    rows.from_across(2)
    rows.from_across(3)
    consume_all(1, (None,))
    consume_all(0, (0, 1))
    rows.from_far(0)
    rows.from_far(1)
    consume_all(0, (2,))
    rows.from_diagonal(0)
    consume_all(1, (0, 1))
    rows.from_far(2)
    rows.from_far(3)
    rows.from_far_across(0)
    consume_all(1, (2,))
    consume_all(0, (3,))
    rows.from_far_across(1)
    rows.from_diagonal(1)
    consume_all(1, (3,))
    consume_all(0, (4, 5, 6))
    rows.from_far_across(2)
    rows.from_diagonal(2)
    rows.from_far_across(3)
    rows.from_diagonal(3)
    consume_all(1, (4, 5, 6))
    kvbuf[ctx, core] = acckv[...].astype(BF16)
    for part in range(2):
        for head in range(2):
            q[head * ROWS + part * HALF : head * ROWS + (part + 1) * HALF, :] = accq[
                part, :, head * HD : (head + 1) * HD
            ].astype(BF16)
    start_ring()

    top[...] = jnp.full_like(top, FAR_BELOW)
    total[...] = jnp.zeros_like(total)
    acc[...] = jnp.zeros_like(acc)
    factor = HD ** (-0.5) * LOG2E

    def attend(keys, values, head, masked):
        at = slice(head * ROWS, (head + 1) * ROWS)
        scores = lax.dot_general(
            q[at, :], keys, (((1,), (1,)), ((), ())), preferred_element_type=F32
        )
        if masked:
            seen = lax.broadcasted_iota(jnp.int32, (ROWS, ROWS), 1) <= lax.broadcasted_iota(
                jnp.int32, (ROWS, ROWS), 0
            )
            scores = jnp.where(seen, scores, FAR_BELOW)
        high = jnp.max(scores, axis=-1, keepdims=True)
        before = top[at, :]
        now = jnp.maximum(before, jnp.broadcast_to(high, (ROWS, 128)))
        decay = jnp.exp2((before - now) * factor)
        shift = now * factor
        weights = []
        for g in range(ROWS // 128):
            lanes = slice(g * 128, (g + 1) * 128)
            part = jnp.exp2(scores[:, lanes] * factor - shift)
            if masked:
                part = jnp.where(seen[:, lanes], part, 0.0)
            weights.append(part)
        total[at, :] = decay * total[at, :] + ((weights[0] + weights[1]) + (weights[2] + weights[3]))
        mixed = jnp.dot(
            jnp.concatenate([part.astype(BF16) for part in weights], axis=1),
            values,
            preferred_element_type=F32,
        )
        acc[at, :] = decay * acc[at, :] + mixed
        top[at, :] = now

    def attend_block(block, masked):
        both = kvbuf[block].reshape(ROWS, 2 * HD)
        for head in range(2):
            attend(both[:, :HD], both[:, HD:], head, masked)

    def units(n):
        d = n // 2 + 1
        its_row = jnp.where(lax.rem(n, 2) == 0, row, 1 - row)

        def one(side, carry):
            valid = (side == 0) | ((side == 1) & (n < 6)) | ((side == 2) & (n == 1))
            block = jnp.where(
                side == 2, other, along(its_row, jnp.where(side == 0, -sense, sense) * d)
            )
            kind = jnp.where(side == 2, 16, jnp.where((side == 0) & (n < 6), 25 + n, 17 + n))

            @pl.when(valid)
            def _():
                klanded(kind, block, 1 - core)

            @pl.when(valid & (block < ctx))
            def _():
                attend_block(block, False)

            return carry

        lax.fori_loop(0, 3, one, 0)

    klanded(15, ctx, 1 - core)
    attend_block(ctx, True)

    def ring_step(k, carry):
        @pl.when(k < 8)
        def _():
            hop(k)

        @pl.when(k > 0)
        def _():
            units(k - 1)

        return carry

    lax.fori_loop(0, 9, ring_step, 0)

    heads = Gather(sbuf, ssend, srecv)
    for p in range(PIECES):
        for head in range(2):
            signs = (2 * sign_ref[head : head + 1, :] - 1).astype(F32)
            at = slice(head * ROWS + p * PROWS, head * ROWS + (p + 1) * PROWS)
            whole = jnp.sum(total[at, :], axis=-1, keepdims=True)
            attended = (acc[at, :] / whole).astype(BF16)
            sbuf[p, me, :, head * HD : (head + 1) * HD] = (
                attended.astype(F32) * signs
            ).astype(BF16)

    for p in (0, 1):
        heads.start_sideways(p)
        heads.start_near(p)
    heads.start_near(2)
    heads.start_near(3)
    load_o.wait()
    load_t.wait()

    def rotate(p):
        heads.mates_landed(p, range(7, 15))

        def strip(i, carry):
            at = pl.ds(pl.multiple_of(i * STRIP, STRIP), STRIP)
            mix = []
            for slot in range(TP):
                both = sbuf[p, slot, at, :].astype(F32)
                mix += [both[:, :HD], both[:, HD:]]
            span = 1
            while span < QH:
                for h in range(QH):
                    if not h & span:
                        a, b = mix[h], mix[h + span]
                        mix[h], mix[h + span] = a + b, a - b
                span *= 2
            for h in range(QH):
                value = mix[h] * QH ** (-0.5)
                limit = CLIP_RATIO * jnp.max(jnp.abs(value), axis=-1, keepdims=True)
                rotated[p, at, h * HD : (h + 1) * HD] = jnp.clip(value, -limit, limit).astype(BF16)
            return carry

        lax.fori_loop(0, PROWS // STRIP, strip, 0)

    heads.from_sides(0)
    heads.from_across(0)
    heads.start_sideways(2)
    heads.start_sideways(3)
    heads.from_sides(1)
    heads.from_across(1)
    heads.from_far(0)
    heads.from_far(1)
    heads.from_diagonal(0)
    heads.from_sides(2)
    heads.from_across(2)
    heads.from_far_across(0)
    heads.from_sides(3)
    heads.from_across(3)
    rotate(0)
    heads.from_far_across(1)
    heads.from_diagonal(1)
    heads.from_far(2)
    heads.from_far(3)
    rotate(1)
    heads.from_diagonal(2)
    heads.from_far_across(2)
    heads.from_diagonal(3)
    heads.from_far_across(3)
    rotate(2)
    rotate(3)
    result = jnp.dot(
        rotated[...].reshape(ROWS, QH * HD), wo[...], preferred_element_type=F32
    )
    branch[...] = result.reshape(PIECES, PROWS, WIDTH)
    box1[me, 0:1, :] = to_lanes(jnp.sum(result * result, axis=1, keepdims=True))

    push_start(box1, psend1, precv1)
    rows.drain(PIECES)
    heads.drain(PIECES)
    share(0, core, 0).wait_send()
    share(128, core, 1).wait_send()

    def drain(kind, carry):
        kcopy(kind, ctx, core, to_mate).wait_send()
        return carry

    lax.fori_loop(0, 31, drain, 0)
    push_wait(box1, psend1, precv1)
    squares = box1[0, 0:1, :]
    for slot in range(1, TP):
        squares = squares + box1[slot, 0:1, :]
    inverse = lax.rsqrt(squares / D + EPS_OUT)
    for p in range(PIECES):
        by_row = to_rows(inverse[:, p * PROWS : (p + 1) * PROWS])
        partial = jnp.zeros((PROWS, 128), F32)
        for g in range(WIDTH // 128):
            lanes = slice(g * 128, (g + 1) * 128)
            normal = branch[p, :, lanes] * by_row
            student[p, :, lanes] = normal.astype(BF16)
            difference = normal - teacher[p, :, lanes].astype(F32)
            partial = partial + difference * difference
        box2[me, 0:1, p * PROWS : (p + 1) * PROWS] = to_lanes(
            jnp.sum(partial, axis=1, keepdims=True)
        )
    push_start(box2, psend2, precv2)
    store = pltpu.make_async_copy(student, student_hbm, x_sem.at[0])
    store.start()
    push_wait(box2, psend2, precv2)
    loss = box2[0, 0:1, :]
    for slot in range(1, TP):
        loss = loss + box2[slot, 0:1, :]
    loss_ref[...] = loss / D
    store.wait()


def block(x, gain, w_query, w_key, w_value, sign_bits, w_out, teacher):
    any_space = pl.BlockSpec(memory_space=pl.ANY)
    vmem = pl.BlockSpec(memory_space=pltpu.VMEM)
    dma = pltpu.SemaphoreType.DMA
    return pl.pallas_call(
        block_kernel,
        out_shape=(
            jax.ShapeDtypeStruct((PIECES, PROWS, WIDTH), BF16),
            jax.ShapeDtypeStruct((1, ROWS), F32),
        ),
        in_specs=[any_space, vmem, any_space, any_space, any_space, vmem, any_space, any_space],
        out_specs=(any_space, vmem),
        scratch_shapes=[
            pltpu.VMEM((PIECES, PROWS, WIDTH), BF16),
            pltpu.VMEM((PIECES, TP, PROWS, WIDTH), BF16),
            pltpu.VMEM((TP, 1, ROWS), F32),
            pltpu.VMEM((D, 256), BF16),
            pltpu.VMEM((256, D), BF16),
            pltpu.VMEM((2, HALF, 256), F32),
            pltpu.VMEM((HALF, 256), F32),
            pltpu.VMEM((QROWS, HD), BF16),
            pltpu.VMEM((16, 2, HALF, 2 * HD), BF16),
            pltpu.VMEM((QROWS, 128), F32),
            pltpu.VMEM((QROWS, 128), F32),
            pltpu.VMEM((QROWS, HD), F32),
            pltpu.VMEM((PIECES, TP, PROWS, 2 * HD), BF16),
            pltpu.VMEM((QH * HD, WIDTH), BF16),
            pltpu.VMEM((PIECES, PROWS, QH * HD), BF16),
            pltpu.VMEM((PIECES, PROWS, WIDTH), F32),
            pltpu.VMEM((PIECES, PROWS, WIDTH), BF16),
            pltpu.VMEM((PIECES, PROWS, WIDTH), BF16),
            pltpu.VMEM((TP, 1, ROWS), F32),
            pltpu.VMEM((TP, 1, ROWS), F32),
            dma((PIECES, 15)),
            dma((PIECES, 15)),
            dma((31,)),
            dma((31,)),
            dma((PIECES, 15)),
            dma((PIECES, 15)),
            dma((TP,)),
            dma((TP,)),
            dma((TP,)),
            dma((TP,)),
            dma((TP,)),
            dma((TP,)),
            dma((2,)),
            dma((2,)),
            dma((5,)),
            dma((PIECES,)),
        ],
        compiler_params=pltpu.CompilerParams(
            collective_id=0, has_side_effects=True, vmem_limit_bytes=VMEM_LIMIT
        ),
        name="block",
    )(
        x.reshape(PIECES, PROWS, WIDTH),
        gain,
        w_query,
        w_key.T,
        w_value.T,
        sign_bits,
        w_out,
        teacher.reshape(PIECES, PROWS, WIDTH),
    )


def hand_over_kernel(student_ref, loss_ref, student_out, loss_out):
    student_out[...] = student_ref[...]
    loss_out[...] = loss_ref[...].reshape(ROWS)


def hand_over(student, loss):
    vmem = pl.BlockSpec(memory_space=pltpu.VMEM)
    return pl.pallas_call(
        hand_over_kernel,
        out_shape=(
            jax.ShapeDtypeStruct((ROWS, WIDTH), BF16),
            jax.ShapeDtypeStruct((ROWS,), F32),
        ),
        in_specs=[vmem, vmem],
        out_specs=(vmem, vmem),
        name="hand_over",
    )(student.reshape(ROWS, WIDTH), loss)


def body(*arguments):
    return hand_over(*block(*arguments))


def solution(mesh):
    in_specs = (
        P("ctx", "tp"),
        P("tp"),
        P(None, "tp"),
        P(None, "tp"),
        P(None, "tp"),
        P("tp", None),
        P(None, "tp"),
        P("ctx", "tp"),
    )
    out_specs = (P("ctx", "tp"), P("ctx"))
    return jax.shard_map(body, mesh=mesh, in_specs=in_specs, out_specs=out_specs, check_vma=False)
```

time: 549 us -> 117 us (0.21); the launches traced: 540 us -> 116 us
  waiting for transfers between devices: 220 us -> 0 us
  Pallas kernels: 0 us -> 116 us
  matrix products: 91.8 us -> 0 us
  other arithmetic: 86.2 us -> 0 us
  blocking collectives: 75.9 us -> 0 us
  local copies, waits for them, and re-layouts: 39.5 us -> 0 us
  between operations: 14.2 us -> 0.64 us
  starting transfers between devices: 11.7 us -> 0 us
    all_gather x4 -> x0, waiting for transfers between devices: 217 us -> none  [the longest x1 83.8 us: body(): block_keys = lax.all_gather(key_vals[0], 'ctx', axis=0, tiled=True)]
    pallas_call x0 -> x2, Pallas kernels: none -> 116 us  [the longest x1 114 us: block(): pl.pallas_call(block_kernel, out_shape=(jax.ShapeDtypeStruct((PIECES, PRO...]
    dot_general x37 -> x0, matrix products: 91.8 us -> none  [the longest x16 44.5 us: advance(): jnp.einsum('kgqn,nkd->kgqd', weights.astype(jnp.bfloat16), values_now, pr...]
    psum x2 -> x0, blocking collectives: 55.8 us -> none  [the longest x1 29 us: body(): row_loss = lax.psum(jnp.sum(difference * difference, axis=-1), 'tp') / D]
    convert_element_type x4 -> x0, other arithmetic: 44.7 us -> none  [the longest x1 35.1 us: body(): quantized = clip_groups(normed).astype(jnp.bfloat16)]
    all_gather x1 -> x0, blocking collectives: 20.1 us -> none  [body(): lax.all_gather(norm_gain, 'tp', axis=0, tiled=True)]
    unnamed x21 -> x0, local copies, waits for them, and re-layouts: 17.8 us -> none
    reduce_sum x18 -> x0, other arithmetic: 14.3 us -> none  [the longest x16 9.01 us: advance(): weight_sum = decay * weight_sum + jnp.sum(weights, axis=-1)]
  transfers between devices with their start and end apart: 6 -> 0, of which waited for: 6 -> 0; matrix products, arithmetic and copies ran while one was open for 3% -> 0% of each run, Pallas kernels for 0% -> 0%
where the time goes in v2:
time: 117 us; the launch traced here: 116 us
  Pallas kernels  116 us (99%)
    pallas_call x1, Pallas kernels, block(): pl.pallas_call(block_kernel, out_shape=(jax.ShapeDtypeStruct((PIECES, PRO...  114 us

profile of v2, /device:TPU:17, one launch (start us, length us, event | category | flops | bytes accessed | tf_op | source)
XLA Modules:
  0.0 116.5 jit_solution(568976673640965781)
XLA Ops:
  0.6 113.9 %block.1 = (bf16[4,128,512]{2,1,0:T(8,128)(2,1)}, f32[1,512]{1,0:T(1,128)}) custom-call(bf16[4,128,512]{2,1,0:T(8,128)(2,1)} %bitcast.7, bf16[512]{0:T(512)(128)(2,1)} %gain_ref.1, bf16[8192,256]{1,0:T(8,128)(2,1)} %wq_hbm.1, bf16[64,8192]{1,0:T(8,128)(2,1)} %bitcast.5, bf16[64,8192]{1,0:T(8,128)(2,1)} %bitcast.6, s32[2,128]{1,0:T(2,128)} %sign_ref.1, ...), custom_call_target="tpu_custom_call" | custom-call | tf_op jit(solution)/shard_map/block/pallas_call | solution.py:600
  114.6 1.9 %hand_over.1 = (bf16[512,512]{1,0:T(8,128)(2,1)}, f32[512]{0:T(512)}) custom-call(bf16[512,512]{1,0:T(8,128)(2,1)} %bitcast.9, f32[1,512]{1,0:T(1,128)} %get-tuple-element.5.loss_ref), custom_call_target="tpu_custom_call" | custom-call | tf_op jit(solution)/shard_map/hand_over/pallas_call | solution.py:669

commit v3 on v2

--- a/solution.py
+++ b/solution.py
@@ -186,7 +186,7 @@
 def block_kernel(
     x_hbm, gain_ref, wq_hbm, wk_hbm, wv_hbm, sign_ref, wo_hbm, teacher_hbm,
     student_hbm, loss_ref,
-    xraw, xbuf, stats, wq, wkv, accq, acckv, q, kvbuf, top, total, acc,
+    xbuf, stats, wq, wkv, inv, accq, acckv, q, kvbuf, top, total, acc,
     sbuf, wo, rotated, branch, teacher, student, box1, box2,
     xsend, xrecv, ksend, krecv, ssend, srecv,
     psend0, precv0, psend1, precv1, psend2, precv2, wsend, wrecv, load_sem, x_sem,
@@ -197,7 +197,7 @@
     core, mate = rows.core, rows.mate
 
     x_loads = [
-        pltpu.make_async_copy(x_hbm.at[p], xraw.at[p], x_sem.at[p]) for p in range(PIECES)
+        pltpu.make_async_copy(x_hbm.at[p], xbuf.at[p, me], x_sem.at[p]) for p in range(PIECES)
     ]
     for load in x_loads:
         load.start()
@@ -236,13 +236,17 @@
 
     for p in range(PIECES):
         x_loads[p].wait()
-        values = xraw[p].astype(F32)
+        values = xbuf[p, me].astype(F32)
         stats[me, 0:1, p * PROWS : (p + 1) * PROWS] = to_lanes(
             jnp.sum(values * values, axis=1, keepdims=True)
         )
+    stats[me, 1:2, :] = gain_ref[...].astype(F32).reshape(1, WIDTH)
     pl.semaphore_wait(barrier, TP - 1 + 3)
 
     push_start(stats, psend0, precv0)
+    for p in range(PIECES):
+        rows.start_sideways(p)
+        rows.start_near(p)
     load_o.start()
     load_t.start()
     load_k.wait()
@@ -265,30 +269,28 @@
     for slot in range(1, TP):
         squares = squares + stats[slot, 0:1, :]
     scale = lax.rsqrt(squares / D + EPS_IN)
-    gain = gain_ref[...].astype(F32).reshape(1, WIDTH)
     for p in range(PIECES):
-        by_row = to_rows(scale[:, p * PROWS : (p + 1) * PROWS])
-        for g in range(WIDTH // 128):
-            lanes = slice(g * 128, (g + 1) * 128)
-            values = xraw[p, :, lanes].astype(F32) * by_row * gain[:, lanes]
-            limit = CLIP_RATIO * jnp.max(jnp.abs(values), axis=-1, keepdims=True)
-            xbuf[p, me, :, lanes] = jnp.clip(values, -limit, limit).astype(BF16)
+        inv[p] = to_rows(scale[:, p * PROWS : (p + 1) * PROWS])
     accq[...] = jnp.zeros_like(accq)
     acckv[...] = jnp.zeros_like(acckv)
 
-    for p in range(PIECES):
-        rows.start_sideways(p)
-        rows.start_near(p)
     load_q.wait()
     share(0, 1 - core, 0).wait_recv()
     share(128, 1 - core, 1).wait_recv()
 
     def consume(part, chip):
         at = pl.ds(pl.multiple_of(chip * 2 * WIDTH, 2 * WIDTH), 2 * WIDTH)
-        both = [
-            jnp.concatenate([xbuf[2 * part, slot], xbuf[2 * part + 1, slot]], axis=0)
-            for slot in (2 * chip, 2 * chip + 1)
-        ]
+        both = []
+        for slot in (2 * chip, 2 * chip + 1):
+            gain = stats[slot, 1:2, :]
+            for g in range(WIDTH // 128):
+                lanes = slice(g * 128, (g + 1) * 128)
+                column = []
+                for p in (2 * part, 2 * part + 1):
+                    values = xbuf[p, slot, :, lanes].astype(F32) * inv[p] * gain[:, lanes]
+                    limit = CLIP_RATIO * jnp.max(jnp.abs(values), axis=-1, keepdims=True)
+                    column.append(jnp.clip(values, -limit, limit).astype(BF16))
+                both.append(jnp.concatenate(column, axis=0))
         quantized = jnp.concatenate(both, axis=1)
         accq[part] += jnp.dot(quantized, wq[at, :], preferred_element_type=F32)
 
@@ -311,55 +313,53 @@
 
         lax.fori_loop(0, len(chips), one, 0)
 
-    def kcopy(kind, block, part, target):
+    def kcopy(kind, block, part, target, g):
         return pltpu.make_async_remote_copy(
-            src_ref=kvbuf.at[block, part],
-            dst_ref=kvbuf.at[block, part],
-            send_sem=ksend.at[kind],
-            recv_sem=krecv.at[kind],
+            src_ref=kvbuf.at[block, part, g],
+            dst_ref=kvbuf.at[block, part, g],
+            send_sem=ksend.at[g, kind],
+            recv_sem=krecv.at[g, kind],
             device_id=target,
             device_id_type=MESH,
         )
 
-    def klanded(kind, block, part):
-        kcopy(kind, block, part, to_mate).wait_recv()
+    def klanded(kind, block, part, g):
+        kcopy(kind, block, part, to_mate, g).wait_recv()
 
     def start_ring():
-        kcopy(1, ctx, core, to_ahead).start()
-        kcopy(9, ctx, core, to_behind).start()
-        kcopy(0, ctx, core, to_other).start()
-        kcopy(15, ctx, core, to_mate).start()
-
-    def hop(n):
-        d = n // 2 + 1
-        its_row = jnp.where(lax.rem(n, 2) == 0, row, 1 - row)
-
-        @pl.when(n == 1)
-        def _():
-            klanded(0, other, core)
-            kcopy(2, other, core, to_ahead).start()
-            kcopy(10, other, core, to_behind).start()
-            kcopy(16, other, core, to_mate).start()
-
-        back = along(its_row, -sense * d)
-        klanded(1 + n, back, core)
-
-        @pl.when(n < 6)
-        def _():
-            kcopy(3 + n, back, core, to_ahead).start()
-
-        kcopy(17 + n, back, core, to_mate).start()
-
-        @pl.when(n < 6)
-        def _():
-            front = along(its_row, sense * d)
-            klanded(9 + n, front, core)
-
-            @pl.when(n < 4)
-            def _():
-                kcopy(11 + n, front, core, to_behind).start()
-
-            kcopy(25 + n, front, core, to_mate).start()
+        for g in range(2):
+            kcopy(0, ctx, core, to_ahead, g).start()
+            kcopy(4, ctx, core, to_behind, g).start()
+            kcopy(7, ctx, core, to_other, g).start()
+            kcopy(15, ctx, core, to_mate, g).start()
+
+    rings = {
+        0: (0, -1, ((1, to_ahead), (8, to_other))),
+        4: (0, 1, ((5, to_behind), (9, to_other))),
+        1: (0, -2, ((2, to_ahead), (10, to_other))),
+        5: (0, 2, ((6, to_behind), (11, to_other))),
+        2: (0, -3, ((3, to_ahead),)),
+        6: (0, 3, ()),
+        3: (0, -4, ()),
+        7: (1, 0, ()),
+        8: (1, -1, ()),
+        9: (1, 1, ()),
+        10: (1, -2, ((12, to_ahead),)),
+        11: (1, 2, ((14, to_behind),)),
+        12: (1, -3, ((13, to_ahead),)),
+        14: (1, 3, ()),
+        13: (1, -4, ()),
+    }
+
+    def pass_on(*kinds):
+        for g in range(2):
+            for kind in kinds:
+                far_row, delta, targets = rings[kind]
+                block = along(1 - row if far_row else row, sense * delta)
+                klanded(kind, block, core, g)
+                for as_kind, target in targets:
+                    kcopy(as_kind, block, core, target, g).start()
+                kcopy(16 + kind, block, core, to_mate, g).start()
 
     rows.from_sides(0)
     rows.from_sides(1)
@@ -391,7 +391,7 @@
     rows.from_far_across(3)
     rows.from_diagonal(3)
     consume_all(1, (4, 5, 6))
-    kvbuf[ctx, core] = acckv[...].astype(BF16)
+    kvbuf[ctx, core] = acckv[...].astype(BF16).reshape(2, PROWS, 2 * HD)
     for part in range(2):
         for head in range(2):
             q[head * ROWS + part * HALF : head * ROWS + (part + 1) * HALF, :] = accq[
@@ -440,44 +440,38 @@
         for head in range(2):
             attend(both[:, :HD], both[:, HD:], head, masked)
 
-    def units(n):
-        d = n // 2 + 1
-        its_row = jnp.where(lax.rem(n, 2) == 0, row, 1 - row)
-
-        def one(side, carry):
-            valid = (side == 0) | ((side == 1) & (n < 6)) | ((side == 2) & (n == 1))
-            block = jnp.where(
-                side == 2, other, along(its_row, jnp.where(side == 0, -sense, sense) * d)
-            )
-            kind = jnp.where(side == 2, 16, jnp.where((side == 0) & (n < 6), 25 + n, 17 + n))
-
-            @pl.when(valid)
-            def _():
-                klanded(kind, block, 1 - core)
-
-            @pl.when(valid & (block < ctx))
-            def _():
-                attend_block(block, False)
-
-            return carry
-
-        lax.fori_loop(0, 3, one, 0)
-
-    klanded(15, ctx, 1 - core)
+    order = (0, 4, 7, 1, 5, 8, 9, 2, 6, 10, 11, 3, 12, 14, 13)
+    twin = {0: 4, 1: 5, 2: 6, 3: 3, 4: 0, 5: 1, 6: 2, 7: 7, 8: 9, 9: 8, 10: 11, 11: 10, 12: 14, 13: 13, 14: 12}
+
+    def unit(j, carry):
+        far_row = pick([jnp.int32(rings[kind][0]) for kind in order], j)
+        delta = pick([jnp.int32(rings[kind][1]) for kind in order], j)
+        kind = pick([jnp.int32(16 + twin[kind]) for kind in order], j)
+        block = along(jnp.where(far_row == 1, 1 - row, row), sense * delta)
+        for g in range(2):
+            klanded(kind, block, 1 - core, g)
+
+        @pl.when(block < ctx)
+        def _():
+            attend_block(block, False)
+
+        return carry
+
+    for g in range(2):
+        klanded(15, ctx, 1 - core, g)
     attend_block(ctx, True)
 
+    steps = ((0, 4), (7, 1, 5), (8, 9, 2, 6), (10, 11, 3), (12, 14), (13,))
+
     def ring_step(k, carry):
-        @pl.when(k < 8)
-        def _():
-            hop(k)
-
-        @pl.when(k > 0)
-        def _():
-            units(k - 1)
-
+        for i, kinds in enumerate(steps):
+            pl.when(k == i)(functools.partial(pass_on, *kinds))
+        low = jnp.maximum(3 * k - 4, 0)
+        high = jnp.minimum(jnp.maximum(3 * k - 1, 0), 15)
+        lax.fori_loop(low, high, unit, 0)
         return carry
 
-    lax.fori_loop(0, 9, ring_step, 0)
+    lax.fori_loop(0, len(steps) + 1, ring_step, 0)
 
     heads = Gather(sbuf, ssend, srecv)
     for p in range(PIECES):
@@ -544,9 +538,9 @@
     rotate(1)
     heads.from_diagonal(2)
     heads.from_far_across(2)
+    rotate(2)
     heads.from_diagonal(3)
     heads.from_far_across(3)
-    rotate(2)
     rotate(3)
     result = jnp.dot(
         rotated[...].reshape(ROWS, QH * HD), wo[...], preferred_element_type=F32
@@ -561,7 +555,8 @@
     share(128, core, 1).wait_send()
 
     def drain(kind, carry):
-        kcopy(kind, ctx, core, to_mate).wait_send()
+        for g in range(2):
+            kcopy(kind, ctx, core, to_mate, g).wait_send()
         return carry
 
     lax.fori_loop(0, 31, drain, 0)
@@ -606,15 +601,15 @@
         in_specs=[any_space, vmem, any_space, any_space, any_space, vmem, any_space, any_space],
         out_specs=(any_space, vmem),
         scratch_shapes=[
-            pltpu.VMEM((PIECES, PROWS, WIDTH), BF16),
             pltpu.VMEM((PIECES, TP, PROWS, WIDTH), BF16),
-            pltpu.VMEM((TP, 1, ROWS), F32),
+            pltpu.VMEM((TP, 2, ROWS), F32),
             pltpu.VMEM((D, 256), BF16),
             pltpu.VMEM((256, D), BF16),
+            pltpu.VMEM((PIECES, PROWS, 128), F32),
             pltpu.VMEM((2, HALF, 256), F32),
             pltpu.VMEM((HALF, 256), F32),
             pltpu.VMEM((QROWS, HD), BF16),
-            pltpu.VMEM((16, 2, HALF, 2 * HD), BF16),
+            pltpu.VMEM((16, 2, 2, PROWS, 2 * HD), BF16),
             pltpu.VMEM((QROWS, 128), F32),
             pltpu.VMEM((QROWS, 128), F32),
             pltpu.VMEM((QROWS, HD), F32),
@@ -628,8 +623,8 @@
             pltpu.VMEM((TP, 1, ROWS), F32),
             dma((PIECES, 15)),
             dma((PIECES, 15)),
-            dma((31,)),
-            dma((31,)),
+            dma((2, 31)),
+            dma((2, 31)),
             dma((PIECES, 15)),
             dma((PIECES, 15)),
             dma((TP,)),

time: 117 us -> 114 us (0.974)
  Pallas kernels: 116 us -> 113 us
    pallas_call x1, Pallas kernels: 114 us -> 111 us  [block(): pl.pallas_call(block_kernel, out_shape=(jax.ShapeDtypeStruct((PIECES, PRO...]
where the time goes in v3:
time: 114 us
  Pallas kernels  113 us (99%)
    pallas_call x1, Pallas kernels, block(): pl.pallas_call(block_kernel, out_shape=(jax.ShapeDtypeStruct((PIECES, PRO...  111 us

profile of v3, /device:TPU:17, one launch (start us, length us, event | category | flops | bytes accessed | tf_op | source)
XLA Modules:
  0.0 113.9 jit_solution(1503414758738770049)
XLA Ops:
  0.6 111.4 %block.1 = (bf16[4,128,512]{2,1,0:T(8,128)(2,1)}, f32[1,512]{1,0:T(1,128)}) custom-call(bf16[4,128,512]{2,1,0:T(8,128)(2,1)} %bitcast.7, bf16[512]{0:T(512)(128)(2,1)} %gain_ref.1, bf16[8192,256]{1,0:T(8,128)(2,1)} %wq_hbm.1, bf16[64,8192]{1,0:T(8,128)(2,1)} %bitcast.5, bf16[64,8192]{1,0:T(8,128)(2,1)} %bitcast.6, s32[2,128]{1,0:T(2,128)} %sign_ref.1, ...), custom_call_target="tpu_custom_call" | custom-call | tf_op jit(solution)/shard_map/block/pallas_call | solution.py:595
  112.0 1.9 %hand_over.1 = (bf16[512,512]{1,0:T(8,128)(2,1)}, f32[512]{0:T(512)}) custom-call(bf16[512,512]{1,0:T(8,128)(2,1)} %bitcast.9, f32[1,512]{1,0:T(1,128)} %get-tuple-element.5.loss_ref), custom_call_target="tpu_custom_call" | custom-call | tf_op jit(solution)/shard_map/hand_over/pallas_call | solution.py:664

commit v4 on v3

--- a/solution.py
+++ b/solution.py
@@ -484,11 +484,9 @@
                 attended.astype(F32) * signs
             ).astype(BF16)
 
-    for p in (0, 1):
+    for p in range(PIECES):
         heads.start_sideways(p)
         heads.start_near(p)
-    heads.start_near(2)
-    heads.start_near(3)
     load_o.wait()
     load_t.wait()
 
@@ -517,30 +515,28 @@
         lax.fori_loop(0, PROWS // STRIP, strip, 0)
 
     heads.from_sides(0)
+    heads.from_sides(1)
     heads.from_across(0)
-    heads.start_sideways(2)
-    heads.start_sideways(3)
-    heads.from_sides(1)
+    heads.from_sides(2)
+    heads.from_sides(3)
     heads.from_across(1)
+    heads.from_across(2)
+    heads.from_across(3)
     heads.from_far(0)
     heads.from_far(1)
     heads.from_diagonal(0)
-    heads.from_sides(2)
-    heads.from_across(2)
-    heads.from_far_across(0)
-    heads.from_sides(3)
-    heads.from_across(3)
-    rotate(0)
-    heads.from_far_across(1)
-    heads.from_diagonal(1)
     heads.from_far(2)
     heads.from_far(3)
+    heads.from_diagonal(1)
+    heads.from_far_across(0)
+    rotate(0)
+    heads.from_diagonal(2)
+    heads.from_far_across(1)
+    heads.from_diagonal(3)
+    heads.from_far_across(2)
     rotate(1)
-    heads.from_diagonal(2)
-    heads.from_far_across(2)
+    heads.from_far_across(3)
     rotate(2)
-    heads.from_diagonal(3)
-    heads.from_far_across(3)
     rotate(3)
     result = jnp.dot(
         rotated[...].reshape(ROWS, QH * HD), wo[...], preferred_element_type=F32

time: 114 us -> 112 us (0.982)
  Pallas kernels: 113 us -> 111 us
    pallas_call x1, Pallas kernels: 111 us -> 109 us  [block(): pl.pallas_call(block_kernel, out_shape=(jax.ShapeDtypeStruct((PIECES, PRO...]
where the time goes in v4:
time: 112 us
  Pallas kernels  111 us (99%)
    pallas_call x1, Pallas kernels, block(): pl.pallas_call(block_kernel, out_shape=(jax.ShapeDtypeStruct((PIECES, PRO...  109 us

profile of v4, /device:TPU:17, one launch (start us, length us, event | category | flops | bytes accessed | tf_op | source)
XLA Modules:
  0.0 111.7 jit_solution(10624354482728428886)
XLA Ops:
  0.6 109.2 %block.1 = (bf16[4,128,512]{2,1,0:T(8,128)(2,1)}, f32[1,512]{1,0:T(1,128)}) custom-call(bf16[4,128,512]{2,1,0:T(8,128)(2,1)} %bitcast.7, bf16[512]{0:T(512)(128)(2,1)} %gain_ref.1, bf16[8192,256]{1,0:T(8,128)(2,1)} %wq_hbm.1, bf16[64,8192]{1,0:T(8,128)(2,1)} %bitcast.5, bf16[64,8192]{1,0:T(8,128)(2,1)} %bitcast.6, s32[2,128]{1,0:T(2,128)} %sign_ref.1, ...), custom_call_target="tpu_custom_call" | custom-call | tf_op jit(solution)/shard_map/block/pallas_call | solution.py:591
  109.8 1.9 %hand_over.1 = (bf16[512,512]{1,0:T(8,128)(2,1)}, f32[512]{0:T(512)}) custom-call(bf16[512,512]{1,0:T(8,128)(2,1)} %bitcast.9, f32[1,512]{1,0:T(1,128)} %get-tuple-element.5.loss_ref), custom_call_target="tpu_custom_call" | custom-call | tf_op jit(solution)/shard_map/hand_over/pallas_call | solution.py:660

commit v5 on v4

--- a/solution.py
+++ b/solution.py
@@ -386,18 +386,26 @@
     rows.from_diagonal(1)
     consume_all(1, (3,))
     consume_all(0, (4, 5, 6))
+
+    def keep_kv():
+        kvbuf[ctx, core] = acckv[...].astype(BF16).reshape(2, PROWS, 2 * HD)
+
+    pl.when(core == 0)(keep_kv)
     rows.from_far_across(2)
     rows.from_diagonal(2)
+    pl.when(core == 0)(start_ring)
     rows.from_far_across(3)
+    consume_all(1, (6,))
     rows.from_diagonal(3)
-    consume_all(1, (4, 5, 6))
-    kvbuf[ctx, core] = acckv[...].astype(BF16).reshape(2, PROWS, 2 * HD)
+    consume_all(1, (4, 5))
+    pl.when(core == 1)(keep_kv)
     for part in range(2):
         for head in range(2):
             q[head * ROWS + part * HALF : head * ROWS + (part + 1) * HALF, :] = accq[
                 part, :, head * HD : (head + 1) * HD
             ].astype(BF16)
-    start_ring()
+    pl.when(core == 1)(start_ring)
+    pl.when(core == 0)(functools.partial(pass_on, 0, 4))
 
     top[...] = jnp.full_like(top, FAR_BELOW)
     total[...] = jnp.zeros_like(total)
@@ -465,7 +473,8 @@
 
     def ring_step(k, carry):
         for i, kinds in enumerate(steps):
-            pl.when(k == i)(functools.partial(pass_on, *kinds))
+            now = (k == i) & (core == 1) if i == 0 else k == i
+            pl.when(now)(functools.partial(pass_on, *kinds))
         low = jnp.maximum(3 * k - 4, 0)
         high = jnp.minimum(jnp.maximum(3 * k - 1, 0), 15)
         lax.fori_loop(low, high, unit, 0)

time: 112 us -> 110 us (0.982)
  Pallas kernels: 111 us -> 109 us
    pallas_call x1, Pallas kernels: 109 us -> 107 us  [block(): pl.pallas_call(block_kernel, out_shape=(jax.ShapeDtypeStruct((PIECES, PRO...]
where the time goes in v5:
time: 110 us; the launch traced here: 109 us
  Pallas kernels  109 us (99%)
    pallas_call x1, Pallas kernels, block(): pl.pallas_call(block_kernel, out_shape=(jax.ShapeDtypeStruct((PIECES, PRO...  107 us

profile of v5, /device:TPU:17, one launch (start us, length us, event | category | flops | bytes accessed | tf_op | source)
XLA Modules:
  0.0 109.5 jit_solution(3199808484427824184)
XLA Ops:
  0.6 106.9 %block.1 = (bf16[4,128,512]{2,1,0:T(8,128)(2,1)}, f32[1,512]{1,0:T(1,128)}) custom-call(bf16[4,128,512]{2,1,0:T(8,128)(2,1)} %bitcast.7, bf16[512]{0:T(512)(128)(2,1)} %gain_ref.1, bf16[8192,256]{1,0:T(8,128)(2,1)} %wq_hbm.1, bf16[64,8192]{1,0:T(8,128)(2,1)} %bitcast.5, bf16[64,8192]{1,0:T(8,128)(2,1)} %bitcast.6, s32[2,128]{1,0:T(2,128)} %sign_ref.1, ...), custom_call_target="tpu_custom_call" | custom-call | tf_op jit(solution)/shard_map/block/pallas_call | solution.py:600
  107.6 1.9 %hand_over.1 = (bf16[512,512]{1,0:T(8,128)(2,1)}, f32[512]{0:T(512)}) custom-call(bf16[512,512]{1,0:T(8,128)(2,1)} %bitcast.9, f32[1,512]{1,0:T(1,128)} %get-tuple-element.5.loss_ref), custom_call_target="tpu_custom_call" | custom-call | tf_op jit(solution)/shard_map/hand_over/pallas_call | solution.py:669

commit v6 on v5

--- a/solution.py
+++ b/solution.py
@@ -397,6 +397,7 @@
     rows.from_far_across(3)
     consume_all(1, (6,))
     rows.from_diagonal(3)
+    pl.when(core == 0)(functools.partial(pass_on, 0, 4))
     consume_all(1, (4, 5))
     pl.when(core == 1)(keep_kv)
     for part in range(2):
@@ -405,7 +406,6 @@
                 part, :, head * HD : (head + 1) * HD
             ].astype(BF16)
     pl.when(core == 1)(start_ring)
-    pl.when(core == 0)(functools.partial(pass_on, 0, 4))
 
     top[...] = jnp.full_like(top, FAR_BELOW)
     total[...] = jnp.zeros_like(total)

time: 110 us -> 108 us (0.982)
  Pallas kernels: 109 us -> 107 us
    pallas_call x1, Pallas kernels: 107 us -> 105 us  [block(): pl.pallas_call(block_kernel, out_shape=(jax.ShapeDtypeStruct((PIECES, PRO...]
where the time goes in v6:
time: 108 us
  Pallas kernels  107 us (99%)
    pallas_call x1, Pallas kernels, block(): pl.pallas_call(block_kernel, out_shape=(jax.ShapeDtypeStruct((PIECES, PRO...  105 us

profile of v6, /device:TPU:17, one launch (start us, length us, event | category | flops | bytes accessed | tf_op | source)
XLA Modules:
  0.0 107.9 jit_solution(11307922142903319816)
XLA Ops:
  0.6 105.4 %block.1 = (bf16[4,128,512]{2,1,0:T(8,128)(2,1)}, f32[1,512]{1,0:T(1,128)}) custom-call(bf16[4,128,512]{2,1,0:T(8,128)(2,1)} %bitcast.7, bf16[512]{0:T(512)(128)(2,1)} %gain_ref.1, bf16[8192,256]{1,0:T(8,128)(2,1)} %wq_hbm.1, bf16[64,8192]{1,0:T(8,128)(2,1)} %bitcast.5, bf16[64,8192]{1,0:T(8,128)(2,1)} %bitcast.6, s32[2,128]{1,0:T(2,128)} %sign_ref.1, ...), custom_call_target="tpu_custom_call" | custom-call | tf_op jit(solution)/shard_map/block/pallas_call | solution.py:600
  106.0 1.9 %hand_over.1 = (bf16[512,512]{1,0:T(8,128)(2,1)}, f32[512]{0:T(512)}) custom-call(bf16[512,512]{1,0:T(8,128)(2,1)} %bitcast.9, f32[1,512]{1,0:T(1,128)} %get-tuple-element.5.loss_ref), custom_call_target="tpu_custom_call" | custom-call | tf_op jit(solution)/shard_map/hand_over/pallas_call | solution.py:669
